TPU v7x, 256 devices: a whole 4x4x8 slice. The times are simulated.
256 devices in a mesh: lead: 8 (over x, core), space: 32 (over z, y).
Axes of the slice: x: 4, y: 4, z: 8, core: 2. Of those that a mesh axis runs over, the one named last changes fastest.
Arguments:
- states: bfloat16 [8, 8, 64, 128, 768], P('lead', None, 'space'), may hold values from -6 to 6
- filter_in: bfloat16 [2, 8, 96, 96], replicated, may hold values from -0.4375 to 0.4375
- filter_out: bfloat16 [2, 8, 96, 96], replicated, may hold values from -0.21875 to 0.21875
- filter_bias: float32 [2, 768], replicated, may hold values from -6 to 6
- decoder: bfloat16 [768, 128], replicated, may hold values from -0.5 to 0.5
- obs_value: float32 [8, 8, 131072], P('lead', None, 'space'), may hold values from -6 to 6
- obs_weight: float32 [8, 131072], P('lead', 'space'), may hold values from 0.5 to 2
- obs_index: int32 [8, 131072], P('lead', 'space'), may hold values from 0 to 32767
- block_dest: int32 [8, 1024], P('lead', 'space'), may hold values from 0 to 31, as said below
- block_count: int32 [8, 1024], P('lead', 'space'), may hold values from 96 to 128
Outputs:
- adjoint_fields: bfloat16 [8, 8, 64, 128, 768], P('lead', None, 'space')
Inputs may be any that keep to these rules, and one draw needn't show every extreme that they name: `block_dest`: at most 2 blocks of one owner in one section name the same tile, and in each section one tile is named by exactly 2 blocks of every owner.
All inputs are finite; a program needn't handle non-finite values.
Results may differ from a plain program's by a relative error of at most 0.017.
Values may be sent and summed in bfloat16 or wider, within the bound.
No kernel may reach another device: no remote copies, remote signals or barrier semaphores. Data moves between devices by JAX's collectives and lax.ppermute only.
A program may use at most 128 MiB of HBM per device.

v0:
```python
import math

import jax
import jax.numpy as jnp
from jax import lax
from jax.sharding import PartitionSpec as P

OBS_BLK = 128


root_scale = math.sqrt(2.0 / math.pi)
cubic_term = 0.044715


def side_by_side(arrays, axis, split_dim, concat_dim, along):
    ends, at = ([], 0)
    for a in arrays[:-1]:
        at += a.shape[along]
        ends.append(at)
    both = jnp.concatenate(arrays, axis=along)
    return tuple(
        jnp.split(
            lax.all_to_all(both, axis, split_axis=split_dim, concat_axis=concat_dim, tiled=True),
            ends,
            axis=along,
        )
    )


def in_one_piece(arrays, axis, split_dim, concat_dim, along):
    columns = [a.reshape(*a.shape[:along], -1) for a in arrays]
    both = jnp.concatenate(columns, axis=along)
    result, at, gathered = (
        lax.all_to_all(both, axis, split_axis=split_dim, concat_axis=concat_dim, tiled=True),
        0,
        [],
    )
    for a, column in zip(arrays, columns):
        piece = result[..., at : at + column.shape[along]]
        gathered.append(piece.reshape(*piece.shape[:along], *a.shape[along:]))
        at += column.shape[along]
    return tuple(gathered)


def gelu_slope(values):
    argument = root_scale * (values + cubic_term * values * values * values)
    tangent = jnp.tanh(argument)
    return 0.5 * (1.0 + tangent) + 0.5 * values * (1.0 - tangent * tangent) * root_scale * (
        1.0 + 3.0 * cubic_term * values * values
    )


def wave_table(row_count, col_count, length):
    row_index = lax.broadcasted_iota(jnp.int32, (row_count, col_count), 0)
    col_index = lax.broadcasted_iota(jnp.int32, (row_count, col_count), 1)
    angles = (row_index * col_index % length).astype(jnp.float32) * (2.0 * math.pi / length)
    return (jnp.cos(angles), jnp.sin(angles))


def make_tables(lon_len, lat_len):
    mode_count = lon_len // 2
    lon_scale = 1.0 / math.sqrt(lon_len)
    lat_scale = 1.0 / math.sqrt(lat_len)
    cos_fore, sin_fore = wave_table(lon_len, mode_count, lon_len)
    cos_back, sin_back = wave_table(mode_count, lon_len, lon_len)
    factor = jnp.where(lax.broadcasted_iota(jnp.int32, (mode_count, 1), 0) == 0, 1.0, 2.0).astype(
        jnp.float32
    )
    cos_lat, sin_lat = wave_table(lat_len, lat_len, lat_len)
    lon_cos = (cos_fore * lon_scale).astype(jnp.bfloat16)
    lon_sin = (-sin_fore * lon_scale).astype(jnp.bfloat16)
    back_cos = (factor * cos_back * lon_scale).astype(jnp.bfloat16)
    back_sin = (-factor * sin_back * lon_scale).astype(jnp.bfloat16)
    lat_cos = (cos_lat * lat_scale).astype(jnp.bfloat16)
    lat_sin = (sin_lat * lat_scale).astype(jnp.bfloat16)
    return (lon_cos, lon_sin, back_cos, back_sin, lat_cos, lat_sin)


def contract(pattern, left_op, right_op):
    return jnp.einsum(pattern, left_op, right_op, preferred_element_type=jnp.float32)


def block_mix(operand, matrix):
    split_view = operand.reshape(operand.shape[:-1] + (matrix.shape[0], matrix.shape[1]))
    return contract("...ni,nio->...no", split_view, matrix).reshape(operand.shape)


def block_mix_t(operand, matrix):
    split_view = operand.reshape(operand.shape[:-1] + (matrix.shape[0], matrix.shape[2]))
    return contract("...no,nio->...ni", split_view, matrix).reshape(operand.shape)


def shards(
    states,
    filter_in,
    filter_out,
    filter_bias,
    decoder,
    obs_value,
    obs_weight,
    obs_index,
    block_dest,
    block_count,
):
    fields = states[0]
    member_count, lat_local, lon_len, channels = fields.shape
    tiles = lax.axis_size("space")
    lon_cos, lon_sin, back_cos, back_sin, lat_cos, lat_sin = make_tables(lon_len, lat_local * tiles)
    spec_re = contract("mfnc,nk->mfkc", fields, lon_cos).astype(jnp.bfloat16)
    spec_im = contract("mfnc,nk->mfkc", fields, lon_sin).astype(jnp.bfloat16)
    piece_re = lax.all_to_all(spec_re, "space", split_axis=2, concat_axis=1, tiled=True)
    piece_im = lax.all_to_all(spec_im, "space", split_axis=2, concat_axis=1, tiled=True)
    mode_re = (
        contract("pf,mfkc->mpkc", lat_cos, piece_re) + contract("pf,mfkc->mpkc", lat_sin, piece_im)
    ).astype(jnp.bfloat16)
    mode_im = (
        contract("pf,mfkc->mpkc", lat_cos, piece_im) - contract("pf,mfkc->mpkc", lat_sin, piece_re)
    ).astype(jnp.bfloat16)
    pre_re = block_mix(mode_re, filter_in[0]) - block_mix(mode_im, filter_in[1]) + filter_bias[0]
    pre_im = block_mix(mode_re, filter_in[1]) + block_mix(mode_im, filter_in[0]) + filter_bias[1]
    slope_re = gelu_slope(pre_re)
    slope_im = gelu_slope(pre_im)
    block_total = block_dest.shape[1]
    slot_cap = 2 * ((block_total + tiles - 1) // tiles)
    live_rows = lax.broadcasted_iota(jnp.int32, (block_total, OBS_BLK), 1) < block_count[0][:, None]
    weight_rows = jnp.where(live_rows, obs_weight[0].reshape(block_total, OBS_BLK), 0.0)
    index_rows = obs_index[0].reshape(block_total, OBS_BLK).astype(jnp.float32)
    value_rows = jnp.swapaxes(obs_value[0].reshape(member_count, block_total, OBS_BLK), 0, 1)
    payload = jnp.concatenate([weight_rows[:, None], index_rows[:, None], value_rows], axis=1)
    targets = block_dest[0]
    matches = (targets[:, None] == lax.broadcasted_iota(jnp.int32, (block_total, tiles), 1)).astype(
        jnp.int32
    )
    earlier = jnp.cumsum(matches, axis=0) - matches
    slot_rank = jnp.sum(earlier * matches, axis=1)
    positions = targets * slot_cap + slot_rank
    outbox = (
        jnp.zeros((tiles * slot_cap, member_count + 2, OBS_BLK), jnp.float32)
        .at[positions]
        .set(payload)
    )
    received = lax.all_to_all(outbox, "space", split_axis=0, concat_axis=0, tiled=True)
    got_weight = received[:, 0].reshape(-1)
    got_index = received[:, 1].reshape(-1).astype(jnp.int32)
    got_value = jnp.swapaxes(received[:, 2:], 0, 1).reshape(member_count, -1)
    levels = decoder.shape[1]
    decoded = contract("mfnc,cv->mfnv", fields, decoder).reshape(member_count, -1)
    innovation = got_weight[None, :] * (decoded[:, got_index] - got_value)
    spread_sum = jnp.zeros_like(decoded).at[:, got_index].add(innovation).astype(jnp.bfloat16)
    forcing = contract(
        "mfnv,cv->mfnc", spread_sum.reshape(member_count, lat_local, lon_len, levels), decoder
    )

    def adjoint_layer(incoming, gain_re, gain_im):
        back_re = contract("mfnc,kn->mfkc", incoming, back_cos).astype(jnp.bfloat16)
        back_im = contract("mfnc,kn->mfkc", incoming, back_sin).astype(jnp.bfloat16)
        wave_re, wave_im = side_by_side((back_re, back_im), "space", 2, 1, 0)
        out_re = (
            contract("fp,mfkc->mpkc", lat_cos, wave_re)
            + contract("fp,mfkc->mpkc", lat_sin, wave_im)
        ).astype(jnp.bfloat16)
        out_im = (
            contract("fp,mfkc->mpkc", lat_cos, wave_im)
            - contract("fp,mfkc->mpkc", lat_sin, wave_re)
        ).astype(jnp.bfloat16)
        hid_re = block_mix_t(out_re, filter_out[0]) + block_mix_t(out_im, filter_out[1])
        hid_im = block_mix_t(out_im, filter_out[0]) - block_mix_t(out_re, filter_out[1])
        act_re = (hid_re * gain_re).astype(jnp.bfloat16)
        act_im = (hid_im * gain_im).astype(jnp.bfloat16)
        grad_re = (block_mix_t(act_re, filter_in[0]) + block_mix_t(act_im, filter_in[1])).astype(
            jnp.bfloat16
        )
        grad_im = (block_mix_t(act_im, filter_in[0]) - block_mix_t(act_re, filter_in[1])).astype(
            jnp.bfloat16
        )
        lat_re = (
            contract("pf,mpkc->mfkc", lat_cos, grad_re)
            - contract("pf,mpkc->mfkc", lat_sin, grad_im)
        ).astype(jnp.bfloat16)
        lat_im = (
            contract("pf,mpkc->mfkc", lat_sin, grad_re)
            + contract("pf,mpkc->mfkc", lat_cos, grad_im)
        ).astype(jnp.bfloat16)
        ret_re, ret_im = side_by_side((lat_re, lat_im), "space", 1, 2, 0)
        return contract("mfkc,nk->mfnc", ret_re, lon_cos) + contract(
            "mfkc,nk->mfnc", ret_im, lon_sin
        )

    lead_count = lax.axis_size("lead")
    moved_forcing, moved_re, moved_im = tuple(
        (
            part.astype(jnp.float32)
            for part in in_one_piece(
                (
                    forcing[None].astype(jnp.bfloat16),
                    slope_re[None].astype(jnp.bfloat16),
                    slope_im[None].astype(jnp.bfloat16),
                ),
                "lead",
                1,
                0,
                2,
            )
        )
    )
    share = member_count // lead_count

    def local_turn(counter, state_pair):
        incoming, result = state_pair
        section = lead_count - 1 - counter
        sec_re = lax.dynamic_index_in_dim(moved_re, section, 0, keepdims=False)
        sec_im = lax.dynamic_index_in_dim(moved_im, section, 0, keepdims=False)
        sec_forcing = lax.dynamic_index_in_dim(moved_forcing, section, 0, keepdims=False)
        updated = (
            incoming.astype(jnp.float32) + adjoint_layer(incoming, sec_re, sec_im) + sec_forcing
        ).astype(jnp.bfloat16)
        return (updated, lax.dynamic_update_index_in_dim(result, updated, section, 0))

    start_field = jnp.zeros((share,) + fields.shape[1:], jnp.bfloat16)
    start_result = jnp.zeros((lead_count, share) + fields.shape[1:], jnp.bfloat16)
    grouped = lax.fori_loop(0, lead_count, local_turn, (start_field, start_result))[1]
    return lax.all_to_all(grouped, "lead", split_axis=0, concat_axis=1, tiled=True)


def solution(mesh):
    placed = (
        P("lead", None, "space", None, None),
        P(),
        P(),
        P(),
        P(),
        P("lead", None, "space"),
        P("lead", "space"),
        P("lead", "space"),
        P("lead", "space"),
        P("lead", "space"),
    )
    return jax.shard_map(
        shards,
        mesh=mesh,
        in_specs=placed,
        out_specs=P("lead", None, "space", None, None),
        check_vma=False,
    )
```

profile of v0, /device:TPU:1, one launch (start us, length us, event | category | flops | bytes accessed | tf_op | source)
XLA Modules:
  0.0 1001.6 jit_solution(9743770898489692489)
XLA Ops:
  5.8 3.8 scatter_fusion
  9.7 12.2 %all-to-all-start.2 = ((f32[64,10,128]{2,1,0:T(8,128)}), f32[64,10,128]{2,1,0:T(8,128)}, u32[]{:S(2)}, u32[]{:S(2)}) async-start(f32[64,10,128]{2,1,0:T(8,128)} %scatter_fusion), calls=%async_computation.2 | async-start | bytes 1048576 | tf_op jit(solution)/shard_map/all_to_all | solution.py:142
  25.3 12.8 %all-to-all-done.2 = f32[64,10,128]{2,1,0:T(8,128)} async-done(((f32[64,10,128]{2,1,0:T(8,128)}), f32[64,10,128]{2,1,0:T(8,128)}, u32[]{:S(2)}, u32[]{:S(2)}) %all-to-all-start.2) | async-done | bytes 327712 | tf_op jit(solution)/shard_map/all_to_all | solution.py:142
  38.1 5.4 all-to-all-start.3
  45.5 9.7 copy.214
  60.3 19.1 %all-to-all-done.3 = bf16[8,2,64,768]{3,1,0,2:T(2,128)(2,1)} async-done(((bf16[8,2,64,768]{3,1,0,2:T(2,128)(2,1)}), bf16[8,2,64,768]{3,1,0,2:T(2,128)(2,1)}, u32[]{:S(2)}, u32[]{:S(2)}) %all-to-all-start.3) | async-done | bytes 1572896 | tf_op jit(solution)/shard_map/all_to_all | solution.py:111
  79.4 8.0 all-to-all-start.4
  88.5 33.6 %gather_fusion = f32[8192,8]{1,0:T(8,128)} fusion(f32[8,32768]{0,1:T(8,128)} %bitcast.471, s32[8192]{0:T(1024)S(1)} %broadcast_clamp_fusion), kind=kCustom, calls=%fused_computation | custom fusion | bytes 557056 | tf_op jit(solution)/shard_map/gather | solution.py:148
  129.6 57.7 %scatter_custom_fusion.1 = f32[8,32768]{0,1:T(8,128)} fusion(s32[8192]{0:T(1024)S(1)} %bitcast.479, f32[8192,8]{1,0:T(8,128)} %copy.182, f32[]{:T(128)} %constant.117.clone.1), kind=kCustom, calls=%fused_computation.196 | custom fusion | flops 65536 | bytes 1049088 | tf_op jit(solution)/shard_map/scatter-add | solution.py:149
  187.3 8.9 convert_element_type.408
  196.2 7.8 copy.183
  206.0 4.5 reshape.847
  224.3 3.8 reshape.783
  236.5 3.9 reshape.784
  243.3 4.3 copy.190
  247.6 6.2 sub.133
  253.8 3.8 fusion.186
  257.7 4.1 copy.195
  262.5 4.3 copy.193
  266.8 6.2 add.400
  278.9 93.6 %fusion.296 = bf16[8,1,393216]{2,1,0:T(2,128)(2,1)} fusion(bf16[1,8,98304]{2,0,1:T(2,128)(2,1)S(1)} %copy.196, bf16[1,8,98304]{2,0,1:T(2,128)(2,1)S(1)} %copy-done.7, bf16[1,8,196608]{2,0,1:T(2,128)(2,1)} %reshape.847), kind=kLoop, calls=%fused_computation.336 | loop fusion | flops 18874368 | bytes 12582912
  373.0 40.1 %reduce.4 = bf16[8,393216]{1,0:T(8,128)(2,1)} reduce(bf16[8,1,393216]{2,1,0:T(2,128)(2,1)} %fusion.296, bf16[]{:T(256)} %broadcast.500), dimensions={1}, to_apply=%fusion.296.reduce_sub_computation | reduce | bytes 12582914
  413.1 11.4 %reshape.854 = bf16[8,2,196608]{2,1,0:T(2,128)(2,1)} reshape(bf16[8,393216]{1,0:T(8,128)(2,1)} %reduce.4) | data formatting | bytes 12582912
  424.5 6.7 all-to-all-start.5
  431.2 71.3 %all-to-all-done.5 = bf16[8,2,196608]{2,1,0:T(2,128)(2,1)} async-done(((bf16[8,2,196608]{2,1,0:T(2,128)(2,1)}), bf16[8,2,196608]{2,1,0:T(2,128)(2,1)}, u32[]{:S(2)}, u32[]{:S(2)}) %all-to-all-start.5) | async-done | bytes 6291488 | tf_op jit(solution)/shard_map/all_to_all | solution.py:34
  502.4 11.0 %reshape.855 = bf16[8,1,393216]{2,1,0:T(2,128)(2,1)} reshape(bf16[8,2,196608]{2,1,0:T(2,128)(2,1)} %all-to-all-done.5) | data formatting | bytes 12582912
  513.4 12.0 %copy.251 = bf16[1,8,393216]{2,1,0:T(8,128)(2,1)S(1)} copy(bf16[1,8,393216]{2,0,1:T(2,128)(2,1)} %bitcast.461) | data formatting | bytes 12582912
  531.7 6.2 reshape.794
  537.9 6.2 reshape.795
  544.1 7.5 copy.225
  553.5 391.5 %while.19 = (s32[]{:T(128)}, bf16[1,2,128,768]{2,3,1,0:T(8,128)(2,1)S(1)}, bf16[8,1,2,128,768]{4,3,2,1,0:T(8,128)(2,1)}, bf16[2,8,96,96]{3,2,1,0:T(8,128)(2,1)S(...) while((s32[]{:T(128)}, ...), condition=%wide.region_5.6_spmd.clone.clone, body=%wide.region_4.5_spmd.clone.clone.sunk | while | flops 357326848 | bytes 39846664 | solution.py:221
  555.6 9.6 all-to-all-start
  567.3 11.7 %all-to-all-done = bf16[2,2,64,768]{3,1,0,2:T(2,128)(2,1)S(1)} async-done(((bf16[2,2,64,768]{3,1,0,2:T(2,128)(2,1)}), bf16[2,2,64,768]{3,1,0,2:T(2,128)(2,1)S(1)}, u32[]{:S(2)}, u32[]{:S(2)}) %all-to-all-start) | async-done | bytes 393248 | tf_op jit(solution)/shard_map/while/body/eval_jaxpr/all_to_all | solution.py:23
  588.6 5.1 all-to-all-start.1
  595.1 11.4 %all-to-all-done.1 = bf16[2,64,2,768]{3,2,0,1:T(2,128)(2,1)S(1)} async-done(((bf16[2,64,2,768]{3,2,0,1:T(2,128)(2,1)}), bf16[2,64,2,768]{3,2,0,1:T(2,128)(2,1)S(1)}, u32[]{:S(2)}, u32[]{:S(2)}) %all-to-all-start.1) | async-done | bytes 393248 | tf_op jit(solution)/shard_map/while/body/eval_jaxpr/all_to_all | solution.py:23
  611.1 5.8 all-to-all-start
  619.0 10.8 %all-to-all-done = bf16[2,2,64,768]{3,1,0,2:T(2,128)(2,1)S(1)} async-done(((bf16[2,2,64,768]{3,1,0,2:T(2,128)(2,1)}), bf16[2,2,64,768]{3,1,0,2:T(2,128)(2,1)S(1)}, u32[]{:S(2)}, u32[]{:S(2)}) %all-to-all-start) | async-done | bytes 393248 | tf_op jit(solution)/shard_map/while/body/eval_jaxpr/all_to_all | solution.py:23
  639.4 5.6 all-to-all-start.1
  646.4 11.1 %all-to-all-done.1 = bf16[2,64,2,768]{3,2,0,1:T(2,128)(2,1)S(1)} async-done(((bf16[2,64,2,768]{3,2,0,1:T(2,128)(2,1)}), bf16[2,64,2,768]{3,2,0,1:T(2,128)(2,1)S(1)}, u32[]{:S(2)}, u32[]{:S(2)}) %all-to-all-start.1) | async-done | bytes 393248 | tf_op jit(solution)/shard_map/while/body/eval_jaxpr/all_to_all | solution.py:23
  662.2 5.8 all-to-all-start
  670.1 10.5 %all-to-all-done = bf16[2,2,64,768]{3,1,0,2:T(2,128)(2,1)S(1)} async-done(((bf16[2,2,64,768]{3,1,0,2:T(2,128)(2,1)}), bf16[2,2,64,768]{3,1,0,2:T(2,128)(2,1)S(1)}, u32[]{:S(2)}, u32[]{:S(2)}) %all-to-all-start) | async-done | bytes 393248 | tf_op jit(solution)/shard_map/while/body/eval_jaxpr/all_to_all | solution.py:23
  690.2 5.7 all-to-all-start.1
  697.4 10.6 %all-to-all-done.1 = bf16[2,64,2,768]{3,2,0,1:T(2,128)(2,1)S(1)} async-done(((bf16[2,64,2,768]{3,2,0,1:T(2,128)(2,1)}), bf16[2,64,2,768]{3,2,0,1:T(2,128)(2,1)S(1)}, u32[]{:S(2)}, u32[]{:S(2)}) %all-to-all-start.1) | async-done | bytes 393248 | tf_op jit(solution)/shard_map/while/body/eval_jaxpr/all_to_all | solution.py:23
  712.5 6.1 all-to-all-start
  720.7 9.8 all-to-all-done
  740.2 6.1 all-to-all-start.1
  747.7 10.3 %all-to-all-done.1 = bf16[2,64,2,768]{3,2,0,1:T(2,128)(2,1)S(1)} async-done(((bf16[2,64,2,768]{3,2,0,1:T(2,128)(2,1)}), bf16[2,64,2,768]{3,2,0,1:T(2,128)(2,1)S(1)}, u32[]{:S(2)}, u32[]{:S(2)}) %all-to-all-start.1) | async-done | bytes 393248 | tf_op jit(solution)/shard_map/while/body/eval_jaxpr/all_to_all | solution.py:23
  762.5 5.7 all-to-all-start
  770.3 9.4 all-to-all-done
  789.3 5.6 all-to-all-start.1
  796.4 10.0 all-to-all-done.1
  811.0 4.6 all-to-all-start
  817.7 9.4 all-to-all-done
  836.8 4.1 all-to-all-start.1
  842.4 10.0 %all-to-all-done.1 = bf16[2,64,2,768]{3,2,0,1:T(2,128)(2,1)S(1)} async-done(((bf16[2,64,2,768]{3,2,0,1:T(2,128)(2,1)}), bf16[2,64,2,768]{3,2,0,1:T(2,128)(2,1)S(1)}, u32[]{:S(2)}, u32[]{:S(2)}) %all-to-all-start.1) | async-done | bytes 393248 | tf_op jit(solution)/shard_map/while/body/eval_jaxpr/all_to_all | solution.py:23
  857.0 3.9 all-to-all-start
  863.0 9.5 all-to-all-done
  882.1 3.9 all-to-all-start.1
  887.4 9.9 all-to-all-done.1
  901.9 3.9 all-to-all-start
  908.0 9.4 all-to-all-done
  927.0 3.9 all-to-all-start.1
  932.4 10.0 all-to-all-done.1
  945.0 53.4 %all_to_all.151 = bf16[8,1,2,128,768]{4,3,2,1,0:T(8,128)(2,1)S(1)} all-to-all(bf16[8,1,2,128,768]{4,3,2,1,0:T(8,128)(2,1)} %get-tuple-element.353), channel_id=1, replica_groups=mesh['lead'=8,'space'=32] {'lead'}, dimensions={0} | all-to-all | bytes 6291456 | tf_op jit(solution)/shard_map/all_to_all | solution.py:222
  (433 shorter events, 209.9 us)
Async XLA Ops:
  0.0 21.8 %copy-start = (bf16[1,8,2,128,768]{4,3,2,1,0:T(8,128)(2,1)S(1)}, bf16[1,8,2,128,768]{4,3,2,1,0:T(8,128)(2,1)}, u32[]{:S(2)}) copy-start(bf16[1,8,2,128,768]{4,3,2,1,0:T(8,128)(2,1)} %param.12) | copy-start | bytes 9437188
  9.7 28.4 %all-to-all-start.2 = ((f32[64,10,128]{2,1,0:T(8,128)}), f32[64,10,128]{2,1,0:T(8,128)}, u32[]{:S(2)}, u32[]{:S(2)}) async-start(f32[64,10,128]{2,1,0:T(8,128)} %scatter_fusion), calls=%async_computation.2 | async-start | bytes 1048576 | tf_op jit(solution)/shard_map/all_to_all | solution.py:142
  22.5 20.9 %copy-start.11 = (bf16[768,128]{1,0:T(8,128)(2,1)S(1)}, bf16[768,128]{1,0:T(8,128)(2,1)}, u32[]{:S(2)}) copy-start(bf16[768,128]{1,0:T(8,128)(2,1)} %param.16) | copy-start | bytes 589828
  38.1 41.3 %all-to-all-start.3 = ((bf16[8,2,64,768]{3,1,0,2:T(2,128)(2,1)}), bf16[8,2,64,768]{3,1,0,2:T(2,128)(2,1)}, u32[]{:S(2)}, u32[]{:S(2)}) async-start(bf16[8,2,64,768]{3,1,0,2:T(2,128)(2,1)} %copy.184), calls=%async_computation.3 | async-start | bytes 3145728 | tf_op jit(solution)/shard_map/all_to_all | solution.py:111
  55.2 3.5 copy-start.12
  79.4 137.0 %all-to-all-start.4 = ((bf16[8,2,64,768]{3,1,0,2:T(2,128)(2,1)}), bf16[8,2,64,768]{3,1,0,2:T(2,128)(2,1)}, u32[]{:S(2)}, u32[]{:S(2)}) async-start(bf16[8,2,64,768]{3,1,0,2:T(2,128)(2,1)} %copy.186), calls=%async_computation.4 | async-start | bytes 3145728 | tf_op jit(solution)/shard_map/all_to_all | solution.py:112
  214.1 5.2 copy-start.5
  219.9 2.5 copy-start.8
  224.3 3.8 copy-start.2
  230.8 2.8 copy-start.6
  230.8 3.9 copy-start.9
  247.6 6.2 copy-start.10
  257.7 4.1 copy-start.4
  276.5 2.4 copy-start.7
  424.5 77.9 %all-to-all-start.5 = ((bf16[8,2,196608]{2,1,0:T(2,128)(2,1)}), bf16[8,2,196608]{2,1,0:T(2,128)(2,1)}, u32[]{:S(2)}, u32[]{:S(2)}) async-start(bf16[8,2,196608]{2,1,0:T(2,128)(2,1)} %reshape.854), calls=%async_computation.5 | async-start | bytes 12582912 | tf_op jit(solution)/shard_map/all_to_all | solution.py:34
  551.6 2.0 copy-start.3
  555.6 23.3 %all-to-all-start = ((bf16[2,2,64,768]{3,1,0,2:T(2,128)(2,1)}), bf16[2,2,64,768]{3,1,0,2:T(2,128)(2,1)S(1)}, u32[]{:S(2)}, u32[]{:S(2)}) async-start(bf16[2,2,64,768]{3,1,0,2:T(2,128)(2,1)} %copy.274), calls=%async_computation | async-start | bytes 786432 | tf_op jit(solution)/shard_map/while/body/eval_jaxpr/all_to_all | solution.py:23
  588.6 18.0 %all-to-all-start.1 = ((bf16[2,64,2,768]{3,2,0,1:T(2,128)(2,1)}), bf16[2,64,2,768]{3,2,0,1:T(2,128)(2,1)S(1)}, u32[]{:S(2)}, u32[]{:S(2)}) async-start(bf16[2,64,2,768]{3,2,0,1:T(2,128)(2,1)} %copy.278), calls=%async_computation.1 | async-start | bytes 786432 | tf_op jit(solution)/shard_map/while/body/eval_jaxpr/all_to_all | solution.py:23
  611.1 18.6 %all-to-all-start = ((bf16[2,2,64,768]{3,1,0,2:T(2,128)(2,1)}), bf16[2,2,64,768]{3,1,0,2:T(2,128)(2,1)S(1)}, u32[]{:S(2)}, u32[]{:S(2)}) async-start(bf16[2,2,64,768]{3,1,0,2:T(2,128)(2,1)} %copy.274), calls=%async_computation | async-start | bytes 786432 | tf_op jit(solution)/shard_map/while/body/eval_jaxpr/all_to_all | solution.py:23
  639.4 18.2 %all-to-all-start.1 = ((bf16[2,64,2,768]{3,2,0,1:T(2,128)(2,1)}), bf16[2,64,2,768]{3,2,0,1:T(2,128)(2,1)S(1)}, u32[]{:S(2)}, u32[]{:S(2)}) async-start(bf16[2,64,2,768]{3,2,0,1:T(2,128)(2,1)} %copy.278), calls=%async_computation.1 | async-start | bytes 786432 | tf_op jit(solution)/shard_map/while/body/eval_jaxpr/all_to_all | solution.py:23
  662.2 18.4 %all-to-all-start = ((bf16[2,2,64,768]{3,1,0,2:T(2,128)(2,1)}), bf16[2,2,64,768]{3,1,0,2:T(2,128)(2,1)S(1)}, u32[]{:S(2)}, u32[]{:S(2)}) async-start(bf16[2,2,64,768]{3,1,0,2:T(2,128)(2,1)} %copy.274), calls=%async_computation | async-start | bytes 786432 | tf_op jit(solution)/shard_map/while/body/eval_jaxpr/all_to_all | solution.py:23
  690.2 17.8 %all-to-all-start.1 = ((bf16[2,64,2,768]{3,2,0,1:T(2,128)(2,1)}), bf16[2,64,2,768]{3,2,0,1:T(2,128)(2,1)S(1)}, u32[]{:S(2)}, u32[]{:S(2)}) async-start(bf16[2,64,2,768]{3,2,0,1:T(2,128)(2,1)} %copy.278), calls=%async_computation.1 | async-start | bytes 786432 | tf_op jit(solution)/shard_map/while/body/eval_jaxpr/all_to_all | solution.py:23
  712.5 18.0 %all-to-all-start = ((bf16[2,2,64,768]{3,1,0,2:T(2,128)(2,1)}), bf16[2,2,64,768]{3,1,0,2:T(2,128)(2,1)S(1)}, u32[]{:S(2)}, u32[]{:S(2)}) async-start(bf16[2,2,64,768]{3,1,0,2:T(2,128)(2,1)} %copy.274), calls=%async_computation | async-start | bytes 786432 | tf_op jit(solution)/shard_map/while/body/eval_jaxpr/all_to_all | solution.py:23
  740.2 17.8 %all-to-all-start.1 = ((bf16[2,64,2,768]{3,2,0,1:T(2,128)(2,1)}), bf16[2,64,2,768]{3,2,0,1:T(2,128)(2,1)S(1)}, u32[]{:S(2)}, u32[]{:S(2)}) async-start(bf16[2,64,2,768]{3,2,0,1:T(2,128)(2,1)} %copy.278), calls=%async_computation.1 | async-start | bytes 786432 | tf_op jit(solution)/shard_map/while/body/eval_jaxpr/all_to_all | solution.py:23
  762.5 17.1 %all-to-all-start = ((bf16[2,2,64,768]{3,1,0,2:T(2,128)(2,1)}), bf16[2,2,64,768]{3,1,0,2:T(2,128)(2,1)S(1)}, u32[]{:S(2)}, u32[]{:S(2)}) async-start(bf16[2,2,64,768]{3,1,0,2:T(2,128)(2,1)} %copy.274), calls=%async_computation | async-start | bytes 786432 | tf_op jit(solution)/shard_map/while/body/eval_jaxpr/all_to_all | solution.py:23
  789.3 17.1 %all-to-all-start.1 = ((bf16[2,64,2,768]{3,2,0,1:T(2,128)(2,1)}), bf16[2,64,2,768]{3,2,0,1:T(2,128)(2,1)S(1)}, u32[]{:S(2)}, u32[]{:S(2)}) async-start(bf16[2,64,2,768]{3,2,0,1:T(2,128)(2,1)} %copy.278), calls=%async_computation.1 | async-start | bytes 786432 | tf_op jit(solution)/shard_map/while/body/eval_jaxpr/all_to_all | solution.py:23
  811.0 16.2 %all-to-all-start = ((bf16[2,2,64,768]{3,1,0,2:T(2,128)(2,1)}), bf16[2,2,64,768]{3,1,0,2:T(2,128)(2,1)S(1)}, u32[]{:S(2)}, u32[]{:S(2)}) async-start(bf16[2,2,64,768]{3,1,0,2:T(2,128)(2,1)} %copy.274), calls=%async_computation | async-start | bytes 786432 | tf_op jit(solution)/shard_map/while/body/eval_jaxpr/all_to_all | solution.py:23
  836.8 15.6 %all-to-all-start.1 = ((bf16[2,64,2,768]{3,2,0,1:T(2,128)(2,1)}), bf16[2,64,2,768]{3,2,0,1:T(2,128)(2,1)S(1)}, u32[]{:S(2)}, u32[]{:S(2)}) async-start(bf16[2,64,2,768]{3,2,0,1:T(2,128)(2,1)} %copy.278), calls=%async_computation.1 | async-start | bytes 786432 | tf_op jit(solution)/shard_map/while/body/eval_jaxpr/all_to_all | solution.py:23
  857.0 15.4 %all-to-all-start = ((bf16[2,2,64,768]{3,1,0,2:T(2,128)(2,1)}), bf16[2,2,64,768]{3,1,0,2:T(2,128)(2,1)S(1)}, u32[]{:S(2)}, u32[]{:S(2)}) async-start(bf16[2,2,64,768]{3,1,0,2:T(2,128)(2,1)} %copy.274), calls=%async_computation | async-start | bytes 786432 | tf_op jit(solution)/shard_map/while/body/eval_jaxpr/all_to_all | solution.py:23
  882.1 15.3 %all-to-all-start.1 = ((bf16[2,64,2,768]{3,2,0,1:T(2,128)(2,1)}), bf16[2,64,2,768]{3,2,0,1:T(2,128)(2,1)S(1)}, u32[]{:S(2)}, u32[]{:S(2)}) async-start(bf16[2,64,2,768]{3,2,0,1:T(2,128)(2,1)} %copy.278), calls=%async_computation.1 | async-start | bytes 786432 | tf_op jit(solution)/shard_map/while/body/eval_jaxpr/all_to_all | solution.py:23
  901.9 15.4 %all-to-all-start = ((bf16[2,2,64,768]{3,1,0,2:T(2,128)(2,1)}), bf16[2,2,64,768]{3,1,0,2:T(2,128)(2,1)S(1)}, u32[]{:S(2)}, u32[]{:S(2)}) async-start(bf16[2,2,64,768]{3,1,0,2:T(2,128)(2,1)} %copy.274), calls=%async_computation | async-start | bytes 786432 | tf_op jit(solution)/shard_map/while/body/eval_jaxpr/all_to_all | solution.py:23
  927.0 15.4 %all-to-all-start.1 = ((bf16[2,64,2,768]{3,2,0,1:T(2,128)(2,1)}), bf16[2,64,2,768]{3,2,0,1:T(2,128)(2,1)S(1)}, u32[]{:S(2)}, u32[]{:S(2)}) async-start(bf16[2,64,2,768]{3,2,0,1:T(2,128)(2,1)} %copy.278), calls=%async_computation.1 | async-start | bytes 786432 | tf_op jit(solution)/shard_map/while/body/eval_jaxpr/all_to_all | solution.py:23
  998.4 3.0 copy-start.1
where the time goes:
time: 1010 us; the launch traced here: 1000 us
  waiting for transfers between devices  267 us (26%)
  local copies, waits for them, and re-layouts  261 us (26%)
  other arithmetic  222 us (22%)
  starting transfers between devices  118 us (12%)
  matrix products  77.8 us (8%)
  blocking collectives  53.4 us (5%)
    all_to_all x16, waiting for transfers between devices, side_by_side(): lax.all_to_all(both, axis, split_axis=split_dim, concat_axis=concat_dim,...  164 us
    unnamed x3, other arithmetic  134 us
    all_to_all x16, starting transfers between devices, side_by_side(): lax.all_to_all(both, axis, split_axis=split_dim, concat_axis=concat_dim,...  85.4 us
    dot_general x172, matrix products, contract(): jnp.einsum(pattern, left_op, right_op, preferred_element_type=jnp.float32)  77.8 us
    all_to_all x1, waiting for transfers between devices, in_one_piece(): lax.all_to_all(both, axis, split_axis=split_dim, concat_axis=concat_dim,...  71.3 us
    scatter-add x1, other arithmetic, shards(): jnp.zeros_like(decoded).at[:, got_index].add(innovation)  57.7 us
    all_to_all x1, blocking collectives, shards(): lax.all_to_all(grouped, 'lead', split_axis=0, concat_axis=1, tiled=True)  53.4 us
    unnamed x32, local copies, waits for them, and re-layouts  46.5 us
  transfers between devices with their start and end apart: 20, of which 19 were waited for; matrix products, arithmetic and copies ran while one was open for 18% of the time, Pallas kernels for 0%

commit v1 on v0

v1 whole, which is shorter than its diff:
```python
import math

import jax
import jax.numpy as jnp
import numpy as np
from jax import lax
from jax.experimental import pallas as pl
from jax.experimental.pallas import tpu as pltpu
from jax.sharding import PartitionSpec as P

OBS_BLK = 128
EVERY = ("lead", "space")

root_scale = math.sqrt(2.0 / math.pi)
cubic_term = 0.044715


def gelu_slope(values):
    square = values * values
    tangent = jnp.tanh(values * (root_scale + (root_scale * cubic_term) * square))
    bend = values * ((0.5 * root_scale) + (1.5 * root_scale * cubic_term) * square)
    return 0.5 + 0.5 * tangent + bend * (1.0 - tangent * tangent)


def waves(rows, cols, length):
    angle = (np.outer(np.arange(rows), np.arange(cols)) % length) * (2.0 * math.pi / length)
    return np.cos(angle), np.sin(angle)


def make_matrices(tiles, lat_local, lon_len):
    lat_len, modes = tiles * lat_local, lon_len // 2
    pair = modes // tiles
    cos, sin = waves(modes, lon_len, lon_len)
    scale = 1.0 / math.sqrt(lon_len)
    gain = np.where(np.arange(modes) == 0, 1.0, 2.0)[:, None]
    nyquist = np.cos(math.pi * np.arange(lon_len)) * scale

    def zonal(factor, full):
        parts = np.stack([factor * cos * scale, -factor * sin * scale])
        parts[1, 0] = nyquist if full else 0.0
        parts = parts.reshape(2, tiles, pair, lon_len).transpose(1, 0, 2, 3)
        out = np.zeros((tiles, lat_local, 2, pair, lat_local, lon_len))
        for f in range(lat_local):
            out[:, f, :, :, f] = parts
        return out.reshape(tiles * lat_local * 2 * pair, lat_local * lon_len)

    lat_cos, lat_sin = (t / math.sqrt(lat_len) for t in waves(lat_len, lat_len, lat_len))
    merid = np.zeros((2, pair, lat_len, lat_len, 2, pair))
    for k in range(pair):
        merid[0, k, :, :, 0, k] = lat_cos
        merid[0, k, :, :, 1, k] = lat_sin
        merid[1, k, :, :, 0, k] = -lat_sin
        merid[1, k, :, :, 1, k] = lat_cos
    merid = merid.reshape(2 * pair * lat_len, lat_len * 2 * pair)
    herm = np.zeros((2, pair, lat_len, 2, pair, lat_len))
    flip = (-np.arange(lat_len)) % lat_len
    for k in range(pair):
        for part in range(2):
            for p in range(lat_len):
                if k == 0:
                    herm[part, k, p, part, k, p] += 0.5
                    herm[part, k, p, part, k, flip[p]] += 0.5 if part == 0 else -0.5
                else:
                    herm[part, k, p, part, k, p] = 1.0
    herm = herm.reshape(2 * pair * lat_len, 2 * pair * lat_len)
    return {
        "state": zonal(1.0, False).astype(np.float32),
        "force": zonal(gain, True).astype(np.float32),
        "back": zonal(1.0, True).T.astype(np.float32),
        "merid": merid.astype(np.float32),
        "merid_t": merid.T.astype(np.float32),
        "herm": herm.astype(np.float32),
    }


def dot(a, b):
    return lax.dot_general(a, b, (((1,), (0,)), ((), ())), preferred_element_type=jnp.float32)


def dot_nt(a, b):
    return lax.dot_general(a, b, (((1,), (1,)), ((), ())), preferred_element_type=jnp.float32)


def mix_rows(matrix, array):
    batch, rows, cols = array.shape
    out_rows = matrix.shape[0]

    def body(m_ref, x_ref, o_ref):
        o_ref[0] = dot(m_ref[...], x_ref[0]).astype(o_ref.dtype)

    return pl.pallas_call(
        body,
        out_shape=jax.ShapeDtypeStruct((batch, out_rows, cols), jnp.bfloat16),
        grid=(batch,),
        in_specs=[
            pl.BlockSpec((out_rows, rows), lambda b: (0, 0)),
            pl.BlockSpec((1, rows, cols), lambda b: (b, 0, 0)),
        ],
        out_specs=pl.BlockSpec((1, out_rows, cols), lambda b: (b, 0, 0)),
        name="mix_rows",
    )(matrix, array)


def pack_outbox(obs_value, obs_weight, obs_index, block_dest, block_count, tiles):
    members, rows = obs_value.shape
    blocks = rows // OBS_BLK

    def body(dest_ref, count_ref, value_ref, weight_ref, index_ref, o_ref, seen_ref):
        o_ref[...] = jnp.zeros_like(o_ref)
        lane = lax.broadcasted_iota(jnp.int32, (1, OBS_BLK), 1)
        for t in range(tiles):
            seen_ref[t] = 0
        for b in range(blocks):
            tile = dest_ref[b]
            rank = seen_ref[tile]
            seen_ref[tile] = rank + 1
            span = slice(b * OBS_BLK, (b + 1) * OBS_BLK)
            weight = jnp.where(lane < count_ref[b], weight_ref[:, span], 0.0)
            o_ref[tile, pl.ds(pl.multiple_of(rank * members, members), members), :] = (
                value_ref[:, span] * weight
            )
            o_ref[tile, pl.ds(2 * members + rank, 1), :] = weight
            o_ref[tile, pl.ds(2 * members + 2 + rank, 1), :] = index_ref[:, span].astype(jnp.float32)

    smem = pl.BlockSpec(memory_space=pltpu.SMEM)
    vmem = pl.BlockSpec(memory_space=pltpu.VMEM)
    return pl.pallas_call(
        body,
        out_shape=jax.ShapeDtypeStruct((tiles, 2 * members + 8, OBS_BLK), jnp.float32),
        in_specs=[smem, smem, vmem, vmem, vmem],
        out_specs=vmem,
        scratch_shapes=[pltpu.SMEM((tiles,), jnp.int32)],
        name="pack_outbox",
    )(block_dest, block_count, obs_value, obs_weight, obs_index)


def level_spectra(received, decoded, matrix):
    sources, rows, lanes = received.shape
    members, cells, levels = decoded.shape
    group = 4
    wide = 2 * lanes
    span = group * wide

    def body(got_ref, dec_ref, mat_ref, o_ref, cell_ref, val_ref, acc_ref):
        acc_ref[...] = jnp.zeros_like(acc_ref)
        cell_iota = lax.broadcasted_iota(jnp.int32, (cells, wide), 0)
        level_iota = lax.broadcasted_iota(jnp.int32, (levels, wide), 0)

        def one_group(g, carry):
            for u in range(group):
                got = got_ref[g * group + u]
                index = jnp.concatenate(
                    [got[2 * members + 2 : 2 * members + 3], got[2 * members + 3 : 2 * members + 4]], axis=1
                ).astype(jnp.int32)
                cell, level = index // levels, index % levels
                first, second = u * wide, span + u * wide
                hot_cell = (cell_iota == cell).astype(jnp.bfloat16)
                cell_ref[:, first : first + wide] = hot_cell
                cell_ref[:, second : second + wide] = hot_cell
                hot_level = (level_iota == level).astype(jnp.bfloat16)
                weight = jnp.concatenate(
                    [got[2 * members : 2 * members + 1], got[2 * members + 1 : 2 * members + 2]], axis=1
                )
                value = jnp.concatenate([got[:members], got[members : 2 * members]], axis=1)
                full = jnp.concatenate([weight, value], axis=0)
                high = full.astype(jnp.bfloat16)
                low = (full - high.astype(jnp.float32)).astype(jnp.bfloat16)
                for q in range(members + 1):
                    at = slice(q * levels, (q + 1) * levels)
                    val_ref[at, first : first + wide] = hot_level * high[q : q + 1]
                    val_ref[at, second : second + wide] = hot_level * low[q : q + 1]
            acc_ref[...] += dot_nt(cell_ref[...], val_ref[...])
            return carry

        lax.fori_loop(0, sources // group, one_group, 0)
        weights = acc_ref[:, :levels]
        for q in range(members):
            forcing = weights * dec_ref[q] - acc_ref[:, (q + 1) * levels : (q + 2) * levels]
            o_ref[q] = dot(mat_ref[...], forcing.astype(jnp.bfloat16)).astype(jnp.bfloat16)

    vmem = pl.BlockSpec(memory_space=pltpu.VMEM)
    return pl.pallas_call(
        body,
        out_shape=jax.ShapeDtypeStruct((members, matrix.shape[0], levels), jnp.bfloat16),
        in_specs=[vmem, vmem, vmem],
        out_specs=vmem,
        scratch_shapes=[
            pltpu.VMEM((cells, 2 * span), jnp.bfloat16),
            pltpu.VMEM(((members + 1) * levels, 2 * span), jnp.bfloat16),
            pltpu.VMEM((cells, (members + 1) * levels), jnp.float32),
        ],
        name="level_spectra",
    )(received, decoded, matrix)


def sweep(spectra, level_spec, merid, merid_t, herm, mats, bias, decoder_t):
    sections, rows, cols = spectra.shape
    levels = level_spec.shape[2]
    chunks, width = mats.shape[1], mats.shape[2]
    half = rows // 2

    def body(x_ref, f_ref, d_ref, dt_ref, h_ref, w_ref, b_ref, dec_ref, o_ref, z_ref):
        @pl.when(pl.program_id(0) == 0)
        def _():
            z_ref[...] = jnp.zeros_like(z_ref)

        forced = dot(d_ref[...], f_ref[0]).astype(jnp.bfloat16)
        for c in range(chunks):
            at = slice(c * width, (c + 1) * width)
            mode = dot(d_ref[...], x_ref[0, :, at]).astype(jnp.bfloat16)
            by_re, by_im = dot(mode, w_ref[0, c]), dot(mode, w_ref[1, c])
            slope_re = gelu_slope(by_re[:half] - by_im[half:] + b_ref[0:1, at])
            slope_im = gelu_slope(by_im[:half] + by_re[half:] + b_ref[1:2, at])
            carry = z_ref[:, at]
            out = dot(h_ref[...], carry.astype(jnp.bfloat16)).astype(jnp.bfloat16)
            by_re, by_im = dot(out, w_ref[2, c]), dot(out, w_ref[3, c])
            act_re = ((by_re[:half] + by_im[half:]) * slope_re).astype(jnp.bfloat16)
            act_im = ((by_re[half:] - by_im[:half]) * slope_im).astype(jnp.bfloat16)
            act = jnp.concatenate([act_re, act_im], axis=0)
            by_re, by_im = dot(act, w_ref[4, c]), dot(act, w_ref[5, c])
            grad = jnp.concatenate(
                [
                    (by_re[:half] + by_im[half:]).astype(jnp.bfloat16),
                    (by_re[half:] - by_im[:half]).astype(jnp.bfloat16),
                ],
                axis=0,
            )
            carry = carry + dot(h_ref[...], grad) + dot(forced, dec_ref[:, at])
            z_ref[:, at] = carry
            o_ref[0, :, at] = dot(dt_ref[...], carry.astype(jnp.bfloat16)).astype(jnp.bfloat16)

    def whole(shape):
        return pl.BlockSpec(shape, lambda t: (0,) * len(shape))

    def turn(shape):
        return pl.BlockSpec(shape, lambda t: (sections - 1 - t, 0, 0))

    return pl.pallas_call(
        body,
        out_shape=jax.ShapeDtypeStruct(spectra.shape, jnp.bfloat16),
        grid=(sections,),
        in_specs=[
            turn((1, rows, cols)),
            turn((1, rows, levels)),
            whole(merid.shape),
            whole(merid_t.shape),
            whole(herm.shape),
            whole(mats.shape),
            whole(bias.shape),
            whole(decoder_t.shape),
        ],
        out_specs=turn((1, rows, cols)),
        scratch_shapes=[pltpu.VMEM((rows, cols), jnp.float32)],
        name="sweep",
    )(spectra, level_spec, merid, merid_t, herm, mats, bias, decoder_t)


def block_diagonal(weights, chunks):
    pieces, blocks, size, _ = weights.shape
    per = blocks // chunks
    split = weights.reshape(pieces, chunks, per, size, 1, size)
    mask = jnp.eye(per, dtype=weights.dtype).reshape(1, 1, per, 1, per, 1)
    return (split * mask).reshape(pieces, chunks, per * size, per * size)


def swap(array, axis):
    batch, rows, cols = array.shape
    return lax.all_to_all(
        array.reshape(-1, 8, cols), axis, split_axis=0, concat_axis=0, tiled=True
    ).reshape(batch, rows, cols)


def shards(
    states,
    filter_in,
    filter_out,
    filter_bias,
    decoder,
    obs_value,
    obs_weight,
    obs_index,
    block_dest,
    block_count,
):
    member_count, lat_local, lon_len, channels = states.shape[1:]
    tiles = lax.axis_size("space")
    tables = {
        name: jnp.asarray(table, jnp.bfloat16)
        for name, table in make_matrices(tiles, lat_local, lon_len).items()
    }
    fields = states.reshape(member_count, lat_local * lon_len, channels)
    outbox = pack_outbox(obs_value[0], obs_weight, obs_index, block_dest[0], block_count[0], tiles)
    received = lax.all_to_all(outbox, "space", split_axis=0, concat_axis=0, tiled=True)
    spectra = swap(mix_rows(tables["state"], fields), EVERY)
    decoded = jnp.einsum("mnc,cv->mnv", fields, decoder, preferred_element_type=jnp.float32)
    levels = swap(level_spectra(received, decoded, tables["force"]), EVERY)
    chunks = 2
    weights = jnp.concatenate(
        [filter_in, jnp.swapaxes(filter_out, 2, 3), jnp.swapaxes(filter_in, 2, 3)], axis=0
    )
    mats = block_diagonal(weights, chunks)
    herm = jnp.where(
        lax.axis_index("space") == 0, tables["herm"], jnp.eye(tables["herm"].shape[0], dtype=jnp.bfloat16)
    )
    swept = sweep(
        spectra, levels, tables["merid"], tables["merid_t"], herm, mats, filter_bias, decoder.T
    )
    result = mix_rows(tables["back"], swap(swept, EVERY))
    return result.reshape(1, member_count, lat_local, lon_len, channels)


def solution(mesh):
    placed = (
        P("lead", None, "space", None, None),
        P(),
        P(),
        P(),
        P(),
        P("lead", None, "space"),
        P("lead", "space"),
        P("lead", "space"),
        P("lead", "space"),
        P("lead", "space"),
    )
    return jax.shard_map(
        shards,
        mesh=mesh,
        in_specs=placed,
        out_specs=P("lead", None, "space", None, None),
        check_vma=False,
    )
```

time: 1010 us -> 278 us (0.28)
  local copies, waits for them, and re-layouts: 261 us -> 17.6 us
  other arithmetic: 222 us -> 4.97 us
  waiting for transfers between devices: 267 us -> 77.4 us
  starting transfers between devices: 118 us -> 29.4 us
  matrix products: 77.8 us -> 3.85 us
  Pallas kernels: 0 us -> 62 us
  blocking collectives: 53.4 us -> 82 us
    all_to_all x19 -> x2, waiting for transfers between devices: 254 us -> 67.5 us  [swap(): lax.all_to_all(array.reshape(-1, 8, cols), axis, split_axis=0, concat_axi...]
    unnamed x3 -> x0, other arithmetic: 134 us -> none
    all_to_all x19 -> x2, starting transfers between devices: 106 us -> 17.3 us  [swap(): lax.all_to_all(array.reshape(-1, 8, cols), axis, split_axis=0, concat_axi...]
    dot_general x172 -> x1, matrix products: 77.8 us -> 3.85 us  [shards(): jnp.einsum('mnc,cv->mnv', fields, decoder, preferred_element_type=jnp.flo...]
    pallas_call x0 -> x5, Pallas kernels: none -> 62 us  [the longest x1 30.9 us: sweep(): pl.pallas_call(body, out_shape=jax.ShapeDtypeStruct(spectra.shape, jnp.bf...]
    scatter-add x1 -> x0, other arithmetic: 57.7 us -> none  [shards(): jnp.zeros_like(decoded).at[:, got_index].add(innovation)]
    unnamed x32 -> x12, local copies, waits for them, and re-layouts: 46.5 us -> 2.66 us
    gather x2 -> x0, local copies, waits for them, and re-layouts: 36.4 us -> none  [shards(): innovation = got_weight[None, :] * (decoded[:, got_index] - got_value)]
  transfers between devices with their start and end apart: 20 -> 3, of which waited for: 19 -> 3; matrix products, arithmetic and copies ran while one was open for 18% -> 9% of each run, Pallas kernels for 0% -> 3%
where the time goes in v1:
time: 278 us; the launch traced here: 277 us
  blocking collectives  82 us (29%)
  waiting for transfers between devices  77.4 us (28%)
  Pallas kernels  62 us (22%)
  starting transfers between devices  29.4 us (11%)
  local copies, waits for them, and re-layouts  17.6 us (6%)
  other arithmetic  4.97 us (2%)
  matrix products  3.85 us (1%)
    all_to_all x1, blocking collectives, swap(): lax.all_to_all(array.reshape(-1, 8, cols), axis, split_axis=0, concat_axi...  82 us
    all_to_all x2, waiting for transfers between devices, swap(): lax.all_to_all(array.reshape(-1, 8, cols), axis, split_axis=0, concat_axi...  67.5 us
    pallas_call x1, Pallas kernels, sweep(): pl.pallas_call(body, out_shape=jax.ShapeDtypeStruct(spectra.shape, jnp.bf...  30.9 us
    all_to_all x2, starting transfers between devices, swap(): lax.all_to_all(array.reshape(-1, 8, cols), axis, split_axis=0, concat_axi...  17.3 us
    pallas_call x1, Pallas kernels, level_spectra(): pl.pallas_call(body, out_shape=jax.ShapeDtypeStruct((members, matrix.shap...  15.4 us
    mul x5, local copies, waits for them, and re-layouts, block_diagonal(): return (split * mask).reshape(pieces, chunks, per * size, per * size)  14.9 us
    pallas_call x2, Pallas kernels, mix_rows(): pl.pallas_call(body, out_shape=jax.ShapeDtypeStruct((batch, out_rows, col...  13.9 us
    all_to_all x1, starting transfers between devices, shards(): lax.all_to_all(outbox, 'space', split_axis=0, concat_axis=0, tiled=True)  12 us
  transfers between devices with their start and end apart: 3, of which 3 were waited for; matrix products, arithmetic and copies ran while one was open for 9% of the time, Pallas kernels for 3%

profile of v1, /device:TPU:1, one launch (start us, length us, event | category | flops | bytes accessed | tf_op | source)
XLA Modules:
  0.0 277.3 jit_solution(6841056298261321008)
XLA Ops:
  0.0 1.8 pack_outbox.1
  1.8 12.0 %all-to-all-start.1 = ((f32[32,24,128]{2,1,0:T(8,128)}), f32[32,24,128]{2,1,0:T(8,128)S(1)}, u32[]{:S(2)}, u32[]{:S(2)}) async-start(f32[32,24,128]{2,1,0:T(8,128)} %pack_outbox.1), calls=%async_computation.1 | async-start | bytes 786432 | tf_op jit(solution)/shard_map/all_to_all | solution.py:293
  13.9 3.8 %fusion.1.dec_ref = f32[8,256,128]{2,1,0:T(8,128)} fusion(bf16[8,256,768]{2,1,0:T(8,128)(2,1)} %bitcast.19, bf16[768,128]{1,0:T(8,128)(2,1)} %param.20), kind=kOutput, calls=%fused_computation.4 | convolution fusion | flops 402653184 | bytes 4390912 | tf_op jit(solution)/shard_map/mnc,cv->mnv/dot_general | solution.py:295
  17.7 10.0 %all-to-all-done.1.got_ref = f32[32,24,128]{2,1,0:T(8,128)S(1)} async-done(((f32[32,24,128]{2,1,0:T(8,128)}), f32[32,24,128]{2,1,0:T(8,128)S(1)}, u32[]{:S(2)}, u32[]{:S(2)}) %all-to-all-start.1) | async-done | bytes 393248 | tf_op jit(solution)/shard_map/all_to_all | solution.py:293
  27.7 0.0 copy-start.2
  27.7 0.7 copy-done.2
  28.4 15.4 %level_spectra.1 = bf16[8,256,128]{2,1,0:T(8,128)(2,1)} custom-call(f32[32,24,128]{2,1,0:T(8,128)} %copy-done.2, f32[8,256,128]{2,1,0:T(8,128)} %fusion.1.dec_ref, bf16[256,256]{1,0:T(8,128)(2,1)} %constant.19.clone.mat_ref), custom_call_target="tpu_custom_call" | custom-call | tf_op jit(solution)/shard_map/level_spectra/pallas_call | solution.py:182
  43.8 9.4 %all-to-all-start.2 = ((bf16[256,8,128]{2,1,0:T(8,128)(2,1)}), bf16[256,8,128]{2,1,0:T(8,128)(2,1)S(1)}, u32[]{:S(2)}, u32[]{:S(2)}) async-start(bf16[256,8,128]{2,1,0:T(8,128)(2,1)} %bitcast.26), calls=%async_computation.2 | async-start | bytes 1048576 | tf_op jit(solution)/shard_map/all_to_all | solution.py:268
  53.2 7.0 %mix_rows.2 = bf16[8,256,768]{2,1,0:T(8,128)(2,1)} custom-call(bf16[256,256]{1,0:T(8,128)(2,1)} %constant.18.clone.m_ref, bf16[8,256,768]{2,1,0:T(8,128)(2,1)} %bitcast.20), custom_call_target="tpu_custom_call" | custom-call | tf_op jit(solution)/shard_map/mix_rows/pallas_call | solution.py:91
  60.2 13.0 %all-to-all-done.2 = bf16[256,8,128]{2,1,0:T(8,128)(2,1)S(1)} async-done(((bf16[256,8,128]{2,1,0:T(8,128)(2,1)}), bf16[256,8,128]{2,1,0:T(8,128)(2,1)S(1)}, u32[]{:S(2)}, u32[]{:S(2)}) %all-to-all-start.2) | async-done | bytes 524320 | tf_op jit(solution)/shard_map/all_to_all | solution.py:268
  73.2 0.0 copy-start
  73.2 0.0 copy-start.3
  73.2 0.0 copy-start.1
  73.2 0.0 copy-start.4
  73.2 0.8 copy-done
  74.1 7.9 %all-to-all-start = ((bf16[256,8,768]{2,1,0:T(8,128)(2,1)}), bf16[256,8,768]{2,1,0:T(8,128)(2,1)}, u32[]{:S(2)}, u32[]{:S(2)}) async-start(bf16[256,8,768]{2,1,0:T(8,128)(2,1)} %bitcast.21), calls=%async_computation | async-start | bytes 6291456 | tf_op jit(solution)/shard_map/all_to_all | solution.py:268
  82.0 0.0 copy-done.3
  82.0 0.8 copy.19
  82.8 0.0 copy-done.1
  82.9 0.2 copy.17
  83.1 0.0 copy-done.4
  83.1 0.3 pad_maximum_fusion
  83.3 0.7 copy.18
  84.0 4.4 %mul.23 = bf16[6,2,4,96,4,96]{5,4,3,2,1,0:T(4,128)(2,1)} broadcast(bf16[6,2,4,96,96]{4,3,2,1,0:T(8,128)(2,1)S(1)} %copy.18), dimensions={0,1,2,3,5} | broadcast | bytes 4423680 | tf_op jit(solution)/shard_map/mul | solution.py:263
  88.4 6.9 %mul.24 = bf16[6,2,384,384]{3,2,1,0:T(8,128)(2,1)S(1)} reshape(bf16[6,2,4,96,4,96]{5,4,3,2,1,0:T(4,128)(2,1)} %mul.23) | data formatting | bytes 7077888 | tf_op jit(solution)/shard_map/mul | solution.py:263
  95.3 0.9 mul.25
  96.3 2.0 mul.26
  98.3 1.6 fusion.3.h_ref
  99.9 3.1 %broadcast_multiply_fusion.w_ref = bf16[6,2,384,384]{3,2,1,0:T(8,128)(2,1)} fusion(bf16[6,2,384,384]{3,2,1,0:T(8,128)(2,1)S(1)} %mul.24, bf16[384,384]{1,0:T(8,128)(2,1)} %mul.26), kind=kLoop, calls=%fused_computation | loop fusion | flops 1769472 | bytes 7372800 | tf_op jit(solution)/shard_map/mul | solution.py:263
  103.0 54.5 %all-to-all-done = bf16[256,8,768]{2,1,0:T(8,128)(2,1)} async-done(((bf16[256,8,768]{2,1,0:T(8,128)(2,1)}), bf16[256,8,768]{2,1,0:T(8,128)(2,1)}, u32[]{:S(2)}, u32[]{:S(2)}) %all-to-all-start) | async-done | bytes 3145760 | tf_op jit(solution)/shard_map/all_to_all | solution.py:268
  157.4 30.9 %sweep.1 = bf16[8,256,768]{2,1,0:T(8,128)(2,1)} custom-call(bf16[8,256,768]{2,1,0:T(8,128)(2,1)} %bitcast.2.x_ref, bf16[8,256,128]{2,1,0:T(8,128)(2,1)} %bitcast.25, bf16[256,256]{1,0:T(8,128)(2,1)} %constant.21.clone.d_ref, bf16[256,256]{1,0:T(8,128)(2,1)} %constant.22.clone.dt_ref, bf16[256,256]{1,0:T(8,128)(2,1)} %fusion.3.h_ref, ...), custom_call_target="tpu_custom_call" | custom-call | tf_op jit(solution)/shard_map/sweep/pallas_call | solution.py:238
  188.3 82.0 %all_to_all.20 = bf16[256,8,768]{2,1,0:T(8,128)(2,1)} all-to-all(bf16[256,8,768]{2,1,0:T(8,128)(2,1)} %bitcast.23), channel_id=1, replica_groups=mesh['lead'=8,'space'=32] {'lead','space'}, dimensions={0} | all-to-all | bytes 6291456 | tf_op jit(solution)/shard_map/all_to_all | solution.py:268
  270.3 7.0 %mix_rows.3 = bf16[8,256,768]{2,1,0:T(8,128)(2,1)} custom-call(bf16[256,256]{1,0:T(8,128)(2,1)} %constant.20.clone.m_ref, bf16[8,256,768]{2,1,0:T(8,128)(2,1)} %bitcast.22), custom_call_target="tpu_custom_call" | custom-call | tf_op jit(solution)/shard_map/mix_rows/pallas_call | solution.py:91
  (1 shorter events, 0.0 us)
Async XLA Ops:
  1.8 25.9 %all-to-all-start.1 = ((f32[32,24,128]{2,1,0:T(8,128)}), f32[32,24,128]{2,1,0:T(8,128)S(1)}, u32[]{:S(2)}, u32[]{:S(2)}) async-start(f32[32,24,128]{2,1,0:T(8,128)} %pack_outbox.1), calls=%async_computation.1 | async-start | bytes 786432 | tf_op jit(solution)/shard_map/all_to_all | solution.py:293
  27.7 0.7 copy-start.2
  43.8 29.4 %all-to-all-start.2 = ((bf16[256,8,128]{2,1,0:T(8,128)(2,1)}), bf16[256,8,128]{2,1,0:T(8,128)(2,1)S(1)}, u32[]{:S(2)}, u32[]{:S(2)}) async-start(bf16[256,8,128]{2,1,0:T(8,128)(2,1)} %bitcast.26), calls=%async_computation.2 | async-start | bytes 1048576 | tf_op jit(solution)/shard_map/all_to_all | solution.py:268
  73.2 0.9 copy-start
  73.2 8.8 %copy-start.3 = (bf16[768,128]{1,0:T(8,128)(2,1)S(1)}, bf16[768,128]{1,0:T(8,128)(2,1)}, u32[]{:S(2)}) copy-start(bf16[768,128]{1,0:T(8,128)(2,1)} %param.20) | copy-start | bytes 589828
  73.2 9.6 %copy-start.1 = (bf16[2,8,96,96]{3,2,1,0:T(8,128)(2,1)S(1)}, bf16[2,8,96,96]{3,2,1,0:T(8,128)(2,1)}, u32[]{:S(2)}) copy-start(bf16[2,8,96,96]{3,2,1,0:T(8,128)(2,1)} %param.17) | copy-start | bytes 884740
  73.2 9.9 %copy-start.4 = (bf16[2,8,96,96]{3,2,1,0:T(8,128)(2,1)S(1)}, bf16[2,8,96,96]{3,2,1,0:T(8,128)(2,1)}, u32[]{:S(2)}) copy-start(bf16[2,8,96,96]{3,2,1,0:T(8,128)(2,1)} %param.18) | copy-start | bytes 884740
  74.1 83.4 %all-to-all-start = ((bf16[256,8,768]{2,1,0:T(8,128)(2,1)}), bf16[256,8,768]{2,1,0:T(8,128)(2,1)}, u32[]{:S(2)}, u32[]{:S(2)}) async-start(bf16[256,8,768]{2,1,0:T(8,128)(2,1)} %bitcast.21), calls=%async_computation | async-start | bytes 6291456 | tf_op jit(solution)/shard_map/all_to_all | solution.py:268

commit v2 on v1

--- a/solution.py
+++ b/solution.py
@@ -81,67 +81,147 @@
     return lax.dot_general(a, b, (((1,), (1,)), ((), ())), preferred_element_type=jnp.float32)
 
 
-def mix_rows(matrix, array):
+def cost(products, moved):
+    return pl.CostEstimate(flops=2 * products, transcendentals=0, bytes_accessed=moved)
+
+
+def mix_rows(matrix, array, per_step=2):
     batch, rows, cols = array.shape
-    out_rows = matrix.shape[0]
 
     def body(m_ref, x_ref, o_ref):
-        o_ref[0] = dot(m_ref[...], x_ref[0]).astype(o_ref.dtype)
-
-    return pl.pallas_call(
-        body,
-        out_shape=jax.ShapeDtypeStruct((batch, out_rows, cols), jnp.bfloat16),
-        grid=(batch,),
-        in_specs=[
-            pl.BlockSpec((out_rows, rows), lambda b: (0, 0)),
-            pl.BlockSpec((1, rows, cols), lambda b: (b, 0, 0)),
-        ],
-        out_specs=pl.BlockSpec((1, out_rows, cols), lambda b: (b, 0, 0)),
+        for u in range(per_step):
+            o_ref[u] = dot(m_ref[...], x_ref[u]).astype(jnp.bfloat16)
+
+    part = pl.BlockSpec((per_step, rows, cols), lambda b: (b, 0, 0))
+    return pl.pallas_call(
+        body,
+        out_shape=jax.ShapeDtypeStruct(array.shape, jnp.bfloat16),
+        grid=(batch // per_step,),
+        in_specs=[pl.BlockSpec((rows, rows), lambda b: (0, 0)), part],
+        out_specs=part,
+        cost_estimate=cost(batch * rows * rows * cols, 4 * batch * rows * cols),
         name="mix_rows",
     )(matrix, array)
 
 
-def pack_outbox(obs_value, obs_weight, obs_index, block_dest, block_count, tiles):
+def dense_blocks(filter_in, filter_out, chunks):
+    _, blocks, size, _ = filter_in.shape
+    per = blocks // chunks
+    width = per * size
+    lift = np.tile(np.eye(size, dtype=np.float32), (per, 1))
+    same = np.kron(np.eye(per, dtype=np.float32), np.ones((size, size), np.float32))
+
+    def body(in_ref, out_ref, lift_ref, same_ref, f_ref, a_ref):
+        same_block = same_ref[...]
+        for c in range(chunks):
+            for q in range(2):
+                at = slice(q * width, (q + 1) * width)
+                w_in = in_ref[q, c * per : (c + 1) * per].reshape(width, size)
+                w_out = out_ref[q, c * per : (c + 1) * per].reshape(width, size)
+                f_ref[0, c, at] = (dot_nt(w_in, lift_ref[...]) * same_block).astype(jnp.bfloat16)
+                a_ref[0, c, at] = (dot_nt(lift_ref[...], w_out) * same_block).astype(jnp.bfloat16)
+                a_ref[1, c, at] = (dot_nt(lift_ref[...], w_in) * same_block).astype(jnp.bfloat16)
+
+    vmem = pl.BlockSpec(memory_space=pltpu.VMEM)
+    return pl.pallas_call(
+        body,
+        out_shape=(
+            jax.ShapeDtypeStruct((1, chunks, 2 * width, width), jnp.bfloat16),
+            jax.ShapeDtypeStruct((2, chunks, 2 * width, width), jnp.bfloat16),
+        ),
+        in_specs=[vmem] * 4,
+        out_specs=(vmem, vmem),
+        cost_estimate=cost(12 * width * width * size, 12 * width * width),
+        name="dense_blocks",
+    )(filter_in, filter_out, jnp.asarray(lift, jnp.bfloat16), jnp.asarray(same, jnp.float32))
+
+
+def pack_outbox(obs_value, obs_weight, obs_index, block_dest, block_count, here, near, far):
     members, rows = obs_value.shape
     blocks = rows // OBS_BLK
-
-    def body(dest_ref, count_ref, value_ref, weight_ref, index_ref, o_ref, seen_ref):
-        o_ref[...] = jnp.zeros_like(o_ref)
+    height = 2 * members + 8
+
+    def body(here_ref, dest_ref, count_ref, value_ref, weight_ref, index_ref, *rest):
+        o_refs, box_ref, seen_ref = rest[:near], rest[near], rest[near + 1]
+        box_ref[...] = jnp.zeros_like(box_ref)
         lane = lax.broadcasted_iota(jnp.int32, (1, OBS_BLK), 1)
-        for t in range(tiles):
+        my_far, my_near = here_ref[0] // near, here_ref[0] % near
+        for t in range(near * far):
             seen_ref[t] = 0
         for b in range(blocks):
             tile = dest_ref[b]
+            slot = (tile % near + near - my_near) % near * far + (tile // near + far - my_far) % far
             rank = seen_ref[tile]
             seen_ref[tile] = rank + 1
             span = slice(b * OBS_BLK, (b + 1) * OBS_BLK)
             weight = jnp.where(lane < count_ref[b], weight_ref[:, span], 0.0)
-            o_ref[tile, pl.ds(pl.multiple_of(rank * members, members), members), :] = (
+            box_ref[slot, pl.ds(pl.multiple_of(rank * members, members), members), :] = (
                 value_ref[:, span] * weight
             )
-            o_ref[tile, pl.ds(2 * members + rank, 1), :] = weight
-            o_ref[tile, pl.ds(2 * members + 2 + rank, 1), :] = index_ref[:, span].astype(jnp.float32)
+            box_ref[slot, pl.ds(2 * members + rank, 1), :] = weight
+            box_ref[slot, pl.ds(2 * members + 2 + rank, 1), :] = index_ref[:, span].astype(jnp.float32)
+        for r in range(near):
+            o_refs[r][...] = box_ref[r * far : (r + 1) * far]
 
     smem = pl.BlockSpec(memory_space=pltpu.SMEM)
     vmem = pl.BlockSpec(memory_space=pltpu.VMEM)
     return pl.pallas_call(
         body,
-        out_shape=jax.ShapeDtypeStruct((tiles, 2 * members + 8, OBS_BLK), jnp.float32),
-        in_specs=[smem, smem, vmem, vmem, vmem],
-        out_specs=vmem,
-        scratch_shapes=[pltpu.SMEM((tiles,), jnp.int32)],
+        out_shape=[jax.ShapeDtypeStruct((far, height, OBS_BLK), jnp.float32)] * near,
+        in_specs=[smem, smem, smem, vmem, vmem, vmem],
+        out_specs=[vmem] * near,
+        scratch_shapes=[
+            pltpu.VMEM((near * far, height, OBS_BLK), jnp.float32),
+            pltpu.SMEM((near * far,), jnp.int32),
+        ],
         name="pack_outbox",
-    )(block_dest, block_count, obs_value, obs_weight, obs_index)
+    )(here, block_dest, block_count, obs_value, obs_weight, obs_index)
+
+
+def regroup(arrays):
+    near, far = len(arrays), arrays[0].shape[0]
+    rest = arrays[0].shape[1:]
+
+    def body(*refs):
+        for q in range(far):
+            for r in range(near):
+                refs[near + q][r] = refs[r][q]
+
+    vmem = pl.BlockSpec(memory_space=pltpu.VMEM)
+    return pl.pallas_call(
+        body,
+        out_shape=[jax.ShapeDtypeStruct((near,) + rest, arrays[0].dtype)] * far,
+        in_specs=[vmem] * near,
+        out_specs=[vmem] * far,
+        name="regroup",
+    )(*arrays)
+
+
+def route(arrays, near, far):
+    def shift(array, by_near, by_far):
+        perm = [
+            (z * near + y, (z + by_far) % far * near + (y + by_near) % near)
+            for z in range(far)
+            for y in range(near)
+        ]
+        return lax.ppermute(array, "space", perm)
+
+    arrays = [arrays[0]] + [shift(arrays[r], r, 0) for r in range(1, near)]
+    arrays = regroup(arrays)
+    return [arrays[0]] + [shift(arrays[q], 0, q) for q in range(1, far)]
 
 
 def level_spectra(received, decoded, matrix):
-    sources, rows, lanes = received.shape
+    parts, group, height, lanes = (len(received),) + received[0].shape
     members, cells, levels = decoded.shape
-    group = 4
     wide = 2 * lanes
     span = group * wide
 
-    def body(got_ref, dec_ref, mat_ref, o_ref, cell_ref, val_ref, acc_ref):
+    def body(*refs):
+        got_refs = refs[:parts]
+        dec_ref, mat_ref, o_ref, got_ref, cell_ref, val_ref, acc_ref = refs[parts:]
+        for q in range(parts):
+            got_ref[q * group : (q + 1) * group] = got_refs[q][...]
         acc_ref[...] = jnp.zeros_like(acc_ref)
         cell_iota = lax.broadcasted_iota(jnp.int32, (cells, wide), 0)
         level_iota = lax.broadcasted_iota(jnp.int32, (levels, wide), 0)
@@ -172,7 +252,7 @@
             acc_ref[...] += dot_nt(cell_ref[...], val_ref[...])
             return carry
 
-        lax.fori_loop(0, sources // group, one_group, 0)
+        lax.fori_loop(0, parts, one_group, 0)
         weights = acc_ref[:, :levels]
         for q in range(members):
             forcing = weights * dec_ref[q] - acc_ref[:, (q + 1) * levels : (q + 2) * levels]
@@ -182,85 +262,105 @@
     return pl.pallas_call(
         body,
         out_shape=jax.ShapeDtypeStruct((members, matrix.shape[0], levels), jnp.bfloat16),
-        in_specs=[vmem, vmem, vmem],
+        in_specs=[vmem] * (parts + 2),
         out_specs=vmem,
         scratch_shapes=[
+            pltpu.VMEM((parts * group, height, lanes), jnp.float32),
             pltpu.VMEM((cells, 2 * span), jnp.bfloat16),
             pltpu.VMEM(((members + 1) * levels, 2 * span), jnp.bfloat16),
             pltpu.VMEM((cells, (members + 1) * levels), jnp.float32),
         ],
+        cost_estimate=cost(16 * parts * group * wide * cells * levels, 4 * members * cells * levels),
         name="level_spectra",
-    )(received, decoded, matrix)
-
-
-def sweep(spectra, level_spec, merid, merid_t, herm, mats, bias, decoder_t):
+    )(*received, decoded, matrix)
+
+
+def slopes(spectra, merid, mats, bias):
     sections, rows, cols = spectra.shape
-    levels = level_spec.shape[2]
-    chunks, width = mats.shape[1], mats.shape[2]
+    _, chunks, _, width = mats.shape
     half = rows // 2
 
-    def body(x_ref, f_ref, d_ref, dt_ref, h_ref, w_ref, b_ref, dec_ref, o_ref, z_ref):
-        @pl.when(pl.program_id(0) == 0)
-        def _():
-            z_ref[...] = jnp.zeros_like(z_ref)
-
-        forced = dot(d_ref[...], f_ref[0]).astype(jnp.bfloat16)
+    def body(x_ref, d_ref, w_ref, b_ref, o_ref):
         for c in range(chunks):
             at = slice(c * width, (c + 1) * width)
             mode = dot(d_ref[...], x_ref[0, :, at]).astype(jnp.bfloat16)
-            by_re, by_im = dot(mode, w_ref[0, c]), dot(mode, w_ref[1, c])
-            slope_re = gelu_slope(by_re[:half] - by_im[half:] + b_ref[0:1, at])
-            slope_im = gelu_slope(by_im[:half] + by_re[half:] + b_ref[1:2, at])
-            carry = z_ref[:, at]
-            out = dot(h_ref[...], carry.astype(jnp.bfloat16)).astype(jnp.bfloat16)
-            by_re, by_im = dot(out, w_ref[2, c]), dot(out, w_ref[3, c])
-            act_re = ((by_re[:half] + by_im[half:]) * slope_re).astype(jnp.bfloat16)
-            act_im = ((by_re[half:] - by_im[:half]) * slope_im).astype(jnp.bfloat16)
-            act = jnp.concatenate([act_re, act_im], axis=0)
-            by_re, by_im = dot(act, w_ref[4, c]), dot(act, w_ref[5, c])
-            grad = jnp.concatenate(
-                [
-                    (by_re[:half] + by_im[half:]).astype(jnp.bfloat16),
-                    (by_re[half:] - by_im[:half]).astype(jnp.bfloat16),
-                ],
-                axis=0,
-            )
-            carry = carry + dot(h_ref[...], grad) + dot(forced, dec_ref[:, at])
-            z_ref[:, at] = carry
-            o_ref[0, :, at] = dot(dt_ref[...], carry.astype(jnp.bfloat16)).astype(jnp.bfloat16)
-
-    def whole(shape):
-        return pl.BlockSpec(shape, lambda t: (0,) * len(shape))
-
-    def turn(shape):
-        return pl.BlockSpec(shape, lambda t: (sections - 1 - t, 0, 0))
-
-    return pl.pallas_call(
-        body,
-        out_shape=jax.ShapeDtypeStruct(spectra.shape, jnp.bfloat16),
+            re, im = mode[:half], mode[half:]
+            pre_re = dot(jnp.concatenate([re, -im], axis=1), w_ref[0, c])
+            pre_im = dot(jnp.concatenate([im, re], axis=1), w_ref[0, c])
+            o_ref[0, :half, at] = gelu_slope(pre_re + b_ref[0:1, at])
+            o_ref[0, half:, at] = gelu_slope(pre_im + b_ref[1:2, at])
+
+    part = pl.BlockSpec((1, rows, cols), lambda t: (t, 0, 0))
+    return pl.pallas_call(
+        body,
+        out_shape=jax.ShapeDtypeStruct(spectra.shape, jnp.float32),
         grid=(sections,),
         in_specs=[
-            turn((1, rows, cols)),
-            turn((1, rows, levels)),
-            whole(merid.shape),
-            whole(merid_t.shape),
-            whole(herm.shape),
-            whole(mats.shape),
-            whole(bias.shape),
-            whole(decoder_t.shape),
+            part,
+            pl.BlockSpec(merid.shape, lambda t: (0, 0)),
+            pl.BlockSpec((1,) + mats.shape[1:], lambda t: (0, 0, 0, 0)),
+            pl.BlockSpec(bias.shape, lambda t: (0, 0)),
         ],
-        out_specs=turn((1, rows, cols)),
-        scratch_shapes=[pltpu.VMEM((rows, cols), jnp.float32)],
+        out_specs=part,
+        cost_estimate=cost(3 * sections * rows * cols * width, 6 * sections * rows * cols),
+        name="slopes",
+    )(spectra, merid, mats, bias)
+
+
+def sweep(slope, level_spec, merid, merid_t, herm, mats, decoder):
+    sections, rows, cols = slope.shape
+    _, chunks, _, width = mats.shape
+    levels = decoder.shape[1]
+    half = rows // 2
+
+    def body(x_ref, f_ref, d_ref, dt_ref, h_ref, w_ref, dec_ref, o_ref, seen_ref, all_ref):
+        @pl.when(pl.program_id(0) == 0)
+        def _():
+            seen_ref[...] = jnp.zeros_like(seen_ref)
+            all_ref[...] = jnp.zeros_like(all_ref)
+
+        def crossed(array):
+            re, im = array[:half], array[half:]
+            return jnp.concatenate(
+                [jnp.concatenate([re, im], axis=1), jnp.concatenate([im, -re], axis=1)], axis=0
+            )
+
+        forced = dot(d_ref[...], f_ref[0]).astype(jnp.bfloat16)
+        forced_seen = dot(h_ref[...], forced).astype(jnp.bfloat16)
+        for c in range(chunks):
+            at = slice(c * width, (c + 1) * width)
+            seen = seen_ref[:, at]
+            hid = dot(crossed(seen.astype(jnp.bfloat16)), w_ref[0, c])
+            act = (hid * x_ref[0, :, at]).astype(jnp.bfloat16)
+            grad = dot(crossed(act), w_ref[1, c]).astype(jnp.bfloat16)
+            grad = dot(h_ref[...], grad)
+            seen_ref[:, at] = seen + grad + dot_nt(forced_seen, dec_ref[at])
+            total = all_ref[:, at] + grad + dot_nt(forced, dec_ref[at])
+            all_ref[:, at] = total
+            o_ref[0, :, at] = dot(dt_ref[...], total.astype(jnp.bfloat16)).astype(jnp.bfloat16)
+
+    def turn(width):
+        return pl.BlockSpec((1, rows, width), lambda t: (sections - 1 - t, 0, 0))
+
+    square = pl.BlockSpec((rows, rows), lambda t: (0, 0))
+    return pl.pallas_call(
+        body,
+        out_shape=jax.ShapeDtypeStruct((sections, rows, cols), jnp.bfloat16),
+        grid=(sections,),
+        in_specs=[
+            turn(cols),
+            turn(levels),
+            square,
+            square,
+            square,
+            pl.BlockSpec((2,) + mats.shape[1:], lambda t: (0, 0, 0, 0)),
+            pl.BlockSpec((cols, levels), lambda t: (0, 0)),
+        ],
+        out_specs=turn(cols),
+        scratch_shapes=[pltpu.VMEM((rows, cols), jnp.float32)] * 2,
+        cost_estimate=cost(6 * sections * rows * cols * width, 6 * sections * rows * cols),
         name="sweep",
-    )(spectra, level_spec, merid, merid_t, herm, mats, bias, decoder_t)
-
-
-def block_diagonal(weights, chunks):
-    pieces, blocks, size, _ = weights.shape
-    per = blocks // chunks
-    split = weights.reshape(pieces, chunks, per, size, 1, size)
-    mask = jnp.eye(per, dtype=weights.dtype).reshape(1, 1, per, 1, per, 1)
-    return (split * mask).reshape(pieces, chunks, per * size, per * size)
+    )(slope, level_spec, merid, merid_t, herm, mats, decoder)
 
 
 def swap(array, axis):
@@ -289,22 +389,22 @@
         for name, table in make_matrices(tiles, lat_local, lon_len).items()
     }
     fields = states.reshape(member_count, lat_local * lon_len, channels)
-    outbox = pack_outbox(obs_value[0], obs_weight, obs_index, block_dest[0], block_count[0], tiles)
-    received = lax.all_to_all(outbox, "space", split_axis=0, concat_axis=0, tiled=True)
+    near = math.gcd(tiles, 4)
+    far = tiles // near
+    here = lax.axis_index("space").astype(jnp.int32)
     spectra = swap(mix_rows(tables["state"], fields), EVERY)
+    outbox = pack_outbox(
+        obs_value[0], obs_weight, obs_index, block_dest[0], block_count[0], here[None], near, far
+    )
+    received = route(outbox, near, far)
     decoded = jnp.einsum("mnc,cv->mnv", fields, decoder, preferred_element_type=jnp.float32)
-    levels = swap(level_spectra(received, decoded, tables["force"]), EVERY)
-    chunks = 2
-    weights = jnp.concatenate(
-        [filter_in, jnp.swapaxes(filter_out, 2, 3), jnp.swapaxes(filter_in, 2, 3)], axis=0
-    )
-    mats = block_diagonal(weights, chunks)
-    herm = jnp.where(
-        lax.axis_index("space") == 0, tables["herm"], jnp.eye(tables["herm"].shape[0], dtype=jnp.bfloat16)
-    )
-    swept = sweep(
-        spectra, levels, tables["merid"], tables["merid_t"], herm, mats, filter_bias, decoder.T
-    )
+    levels = level_spectra(received, decoded, tables["force"])
+    spectra, levels = lax.optimization_barrier((spectra, levels))
+    levels = swap(levels, EVERY)
+    forward, adjoint = dense_blocks(filter_in, filter_out, 2)
+    herm = jnp.where(here == 0, tables["herm"], jnp.eye(tables["herm"].shape[0], dtype=jnp.bfloat16))
+    slope = slopes(spectra, tables["merid"], forward, filter_bias)
+    swept = sweep(slope, levels, tables["merid"], tables["merid_t"], herm, adjoint, decoder)
     result = mix_rows(tables["back"], swap(swept, EVERY))
     return result.reshape(1, member_count, lat_local, lon_len, channels)
 

time: 278 us -> 262 us (0.942)
  waiting for transfers between devices: 77.4 us -> 57 us
  starting transfers between devices: 29.4 us -> 46.6 us
  local copies, waits for them, and re-layouts: 17.6 us -> 2.72 us
  other arithmetic: 4.97 us -> 0.69 us
  Pallas kernels: 62 us -> 66.2 us
  blocking collectives: 82 us -> 86.1 us
    all_to_all x2, waiting for transfers between devices: 67.5 us -> 3.85 us  [swap(): lax.all_to_all(array.reshape(-1, 8, cols), axis, split_axis=0, concat_axi...]
    ppermute x0 -> x10, waiting for transfers between devices: none -> 53.1 us  [shift(): return lax.ppermute(array, 'space', perm)]
    ppermute x0 -> x10, starting transfers between devices: none -> 20.6 us  [shift(): return lax.ppermute(array, 'space', perm)]
    mul x5 -> x0, local copies, waits for them, and re-layouts: 14.9 us -> none  [block_diagonal(): return (split * mask).reshape(pieces, chunks, per * size, per * size)]
    all_to_all x1 -> x0, starting transfers between devices: 12 us -> none  [shards(): lax.all_to_all(outbox, 'space', split_axis=0, concat_axis=0, tiled=True)]
    all_to_all x1 -> x0, waiting for transfers between devices: 9.97 us -> none  [shards(): lax.all_to_all(outbox, 'space', split_axis=0, concat_axis=0, tiled=True)]
    all_to_all x2, starting transfers between devices: 17.3 us -> 26 us  [swap(): lax.all_to_all(array.reshape(-1, 8, cols), axis, split_axis=0, concat_axi...]
    all_to_all x1, blocking collectives: 82 us -> 86.1 us  [swap(): lax.all_to_all(array.reshape(-1, 8, cols), axis, split_axis=0, concat_axi...]
  transfers between devices with their start and end apart: 3 -> 12, of which waited for: 3 -> 6; matrix products, arithmetic and copies ran while one was open for 9% -> 1% of each run, Pallas kernels for 3% -> 13%
where the time goes in v2:
time: 262 us; the launch traced here: 261 us
  blocking collectives  86.1 us (33%)
  Pallas kernels  66.2 us (25%)
  waiting for transfers between devices  57 us (22%)
  starting transfers between devices  46.6 us (18%)
  local copies, waits for them, and re-layouts  2.72 us (1%)
    all_to_all x1, blocking collectives, swap(): lax.all_to_all(array.reshape(-1, 8, cols), axis, split_axis=0, concat_axi...  86.1 us
    ppermute x10, waiting for transfers between devices, shift(): return lax.ppermute(array, 'space', perm)  53.1 us
    all_to_all x2, starting transfers between devices, swap(): lax.all_to_all(array.reshape(-1, 8, cols), axis, split_axis=0, concat_axi...  26 us
    pallas_call x1, Pallas kernels, sweep(): pl.pallas_call(body, out_shape=jax.ShapeDtypeStruct((sections, rows, cols...  21.5 us
    ppermute x10, starting transfers between devices, shift(): return lax.ppermute(array, 'space', perm)  20.6 us
    pallas_call x1, Pallas kernels, level_spectra(): pl.pallas_call(body, out_shape=jax.ShapeDtypeStruct((members, matrix.shap...  15.6 us
    pallas_call x1, Pallas kernels, slopes(): pl.pallas_call(body, out_shape=jax.ShapeDtypeStruct(spectra.shape, jnp.fl...  11.4 us
    pallas_call x2, Pallas kernels, mix_rows(): pl.pallas_call(body, out_shape=jax.ShapeDtypeStruct(array.shape, jnp.bflo...  9.75 us
  transfers between devices with their start and end apart: 12, of which 6 were waited for; matrix products, arithmetic and copies ran while one was open for 1% of the time, Pallas kernels for 13%

profile of v2, /device:TPU:1, one launch (start us, length us, event | category | flops | bytes accessed | tf_op | source)
XLA Modules:
  0.0 261.3 jit_solution(17086962405742616007)
XLA Ops:
  0.0 4.9 %mix_rows.2 = bf16[8,256,768]{2,1,0:T(8,128)(2,1)} custom-call(bf16[256,256]{1,0:T(8,128)(2,1)} %constant.22.clone.m_ref, bf16[8,256,768]{2,1,0:T(8,128)(2,1)} %bitcast.16), custom_call_target="tpu_custom_call" | custom-call | flops 805306368 | bytes 6291456 | tf_op jit(solution)/shard_map/mix_rows/pallas_call | solution.py:96
  4.9 0.0 copy-start
  4.9 0.0 copy-start.2
  4.9 16.5 %all-to-all-start = ((bf16[256,8,768]{2,1,0:T(8,128)(2,1)}), bf16[256,8,768]{2,1,0:T(8,128)(2,1)}, u32[]{:S(2)}, u32[]{:S(2)}) async-start(bf16[256,8,768]{2,1,0:T(8,128)(2,1)} %bitcast.18), calls=%async_computation | async-start | bytes 6291456 | tf_op jit(solution)/shard_map/all_to_all | solution.py:368
  21.4 2.2 pack_outbox.1
  23.6 1.4 collective-permute-start
  25.0 2.5 collective-permute-start.1
  27.4 1.1 collective-permute-start.2
  28.5 4.6 %collective-permute-done.refs_1_ = f32[8,24,128]{2,1,0:T(8,128)S(1)} collective-permute-done((f32[8,24,128]{2,1,0:T(8,128)}, f32[8,24,128]{2,1,0:T(8,128)S(1)}, u32[]{:S(2)}, u32[]{:S(2)}) %collective-permute-start) | collective-permute-done | bytes 98336 | tf_op jit(solution)/shard_map/ppermute | solution.py:207
  33.1 0.0 copy-start.4
  33.1 4.9 %collective-permute-done.1.refs_2_ = f32[8,24,128]{2,1,0:T(8,128)S(1)} collective-permute-done((f32[8,24,128]{2,1,0:T(8,128)}, f32[8,24,128]{2,1,0:T(8,128)S(1)}, u32[]{:S(2)}, u32[]{:S(2)}) %collective-permute-start.1) | collective-permute-done | bytes 98336 | tf_op jit(solution)/shard_map/ppermute | solution.py:207
  38.0 0.0 copy-start.5
  38.0 0.0 collective-permute-done.2.refs_3_
  38.0 0.0 copy-done.4
  38.0 0.6 copy-done.5
  38.6 1.8 regroup.1
  40.4 1.3 collective-permute-start.3
  41.7 3.2 %collective-permute-start.4 = (f32[4,24,128]{2,1,0:T(8,128)}, f32[4,24,128]{2,1,0:T(8,128)S(1)}, u32[]{:S(2)}, u32[]{:S(2)}) collective-permute-start(f32[4,24,128]{2,1,0:T(8,128)} %get-tuple-element.27), channel_id=1, source_target_pairs={{0,8},{1,9},{2,10},{3,11},{4,12},{5,13},{6,14},{7,15},{8,16},{9,17... | collective-permute-start | bytes 147464 | tf_op jit(solution)/shard_map/ppermute | solution.py:207
  44.9 4.2 %collective-permute-start.5 = (f32[4,24,128]{2,1,0:T(8,128)}, f32[4,24,128]{2,1,0:T(8,128)S(1)}, u32[]{:S(2)}, u32[]{:S(2)}) collective-permute-start(f32[4,24,128]{2,1,0:T(8,128)} %get-tuple-element.28), channel_id=1, source_target_pairs={{0,12},{1,13},{2,14},{3,15},{4,16},{5,17},{6,18},{7,19},{8,20},{9,... | collective-permute-start | bytes 147464 | tf_op jit(solution)/shard_map/ppermute | solution.py:207
  49.1 0.2 collective-permute-start.6
  49.4 4.5 %collective-permute-start.7 = (f32[4,24,128]{2,1,0:T(8,128)}, f32[4,24,128]{2,1,0:T(8,128)S(1)}, u32[]{:S(2)}, u32[]{:S(2)}) collective-permute-start(f32[4,24,128]{2,1,0:T(8,128)} %get-tuple-element.30), channel_id=1, source_target_pairs={{0,20},{1,21},{2,22},{3,23},{4,24},{5,25},{6,26},{7,27},{8,28},{9,... | collective-permute-start | bytes 147464 | tf_op jit(solution)/shard_map/ppermute | solution.py:207
  53.8 38.1 %collective-permute-done.3.refs_1_ = f32[4,24,128]{2,1,0:T(8,128)S(1)} collective-permute-done((f32[4,24,128]{2,1,0:T(8,128)}, f32[4,24,128]{2,1,0:T(8,128)S(1)}, u32[]{:S(2)}, u32[]{:S(2)}) %collective-permute-start.3) | collective-permute-done | bytes 49184 | tf_op jit(solution)/shard_map/ppermute | solution.py:207
  91.9 0.0 copy-start.6
  91.9 1.6 collective-permute-start.8
  93.6 0.9 collective-permute-done.4.refs_2_
  94.5 0.0 copy-start.7
  94.5 0.6 collective-permute-start.9
  95.2 0.0 copy-done
  95.2 0.0 copy-done.2
  95.2 2.0 fusion.1.refs_8_
  97.1 0.0 collective-permute-done.5.refs_3_
  97.1 0.0 copy-start.8
  97.1 4.6 %collective-permute-done.6.refs_4_ = f32[4,24,128]{2,1,0:T(8,128)S(1)} collective-permute-done((f32[4,24,128]{2,1,0:T(8,128)}, f32[4,24,128]{2,1,0:T(8,128)S(1)}, u32[]{:S(2)}, u32[]{:S(2)}) %collective-permute-start.6) | collective-permute-done | bytes 49184 | tf_op jit(solution)/shard_map/ppermute | solution.py:207
  101.8 0.0 copy-start.9
  101.8 0.0 collective-permute-done.7.refs_5_
  101.8 0.0 copy-start.10
  101.8 0.0 collective-permute-done.8.refs_6_
  101.8 0.0 copy-start.11
  101.8 0.0 collective-permute-done.9.refs_7_
  101.8 0.6 copy-done.10
  102.4 0.0 copy-done.11
  102.4 0.0 copy-start.12
  102.4 0.6 copy-done.12
  103.1 0.0 copy-done.6
  103.1 0.0 copy-done.7
  103.1 0.0 copy-done.8
  103.1 0.0 copy-done.9
  103.1 0.0 copy-start.3
  103.1 15.6 %level_spectra.1 = bf16[8,256,128]{2,1,0:T(8,128)(2,1)} custom-call(f32[4,24,128]{2,1,0:T(8,128)} %get-tuple-element.25.refs_0_, f32[4,24,128]{2,1,0:T(8,128)} %copy-done.6, f32[4,24,128]{2,1,0:T(8,128)} %copy-done.7, f32[4,24,128]{2,1,0:T(8,128)} %copy-done.8, f32[4,24,128]{2,1,0:T(8,128)} %copy-done.9, f32[4,24,128]{2,1,0:T(8,128)} %copy-done.10, ...), custom_call_target="tpu_custom_call" | custom-call | flops 8589934592 | bytes 1048576 | tf_op jit(solution)/shard_map/level_spectra/pallas_call | solution.py:262
  118.6 0.0 all-to-all-done
  118.6 9.5 %all-to-all-start.1 = ((bf16[256,8,128]{2,1,0:T(8,128)(2,1)}), bf16[256,8,128]{2,1,0:T(8,128)(2,1)S(1)}, u32[]{:S(2)}, u32[]{:S(2)}) async-start(bf16[256,8,128]{2,1,0:T(8,128)(2,1)} %bitcast.21), calls=%async_computation.1 | async-start | bytes 1048576 | tf_op jit(solution)/shard_map/all_to_all | solution.py:368
  128.1 4.1 %dense_blocks.1 = (bf16[1,2,768,384]{3,2,1,0:T(8,128)(2,1)}, bf16[2,2,768,384]{3,2,1,0:T(8,128)(2,1)}) custom-call(bf16[2,8,96,96]{3,2,1,0:T(8,128)(2,1)} %in_ref.1, bf16[2,8,96,96]{3,2,1,0:T(8,128)(2,1)} %out_ref.1, bf16[384,96]{1,0:T(8,128)(2,1)} %constant.28.clone.lift_ref, f32[384,384]{1,0:T(8,128)} %constant.29.clone.same_ref), custom_call_target="tpu_custom_call" | custom-call | flops 339738624 | bytes 1769472 | tf_op jit(solution)/shard_map/dense_blocks/pallas_call | solution.py:126
  132.2 0.0 copy-done.3
  132.2 0.7 fusion.3.h_ref
  132.9 11.4 %slopes.1.x_ref = f32[8,256,768]{2,1,0:T(8,128)} custom-call(bf16[8,256,768]{2,1,0:T(8,128)(2,1)} %bitcast.2.x_ref, bf16[256,256]{1,0:T(8,128)(2,1)} %constant.25.clone.d_ref, bf16[1,2,768,384]{3,2,1,0:T(8,128)(2,1)} %get-tuple-element.34.w_ref, f32[2,768]{1,0:T(2,128)} %b_ref.1), custom_call_target="tpu_custom_call" | custom-call | flops 3623878656 | bytes 9437184 | tf_op jit(solution)/shard_map/slopes/pallas_call | solution.py:294
  144.2 3.8 %all-to-all-done.1 = bf16[256,8,128]{2,1,0:T(8,128)(2,1)S(1)} async-done(((bf16[256,8,128]{2,1,0:T(8,128)(2,1)}), bf16[256,8,128]{2,1,0:T(8,128)(2,1)S(1)}, u32[]{:S(2)}, u32[]{:S(2)}) %all-to-all-start.1) | async-done | bytes 524320 | tf_op jit(solution)/shard_map/all_to_all | solution.py:368
  148.1 0.0 copy-start.1
  148.1 0.8 copy-done.1
  148.9 21.5 %sweep.1 = bf16[8,256,768]{2,1,0:T(8,128)(2,1)} custom-call(f32[8,256,768]{2,1,0:T(8,128)} %slopes.1.x_ref, bf16[8,256,128]{2,1,0:T(8,128)(2,1)} %bitcast.22, bf16[256,256]{1,0:T(8,128)(2,1)} %constant.25.clone.d_ref, bf16[256,256]{1,0:T(8,128)(2,1)} %constant.26.clone.dt_ref, bf16[256,256]{1,0:T(8,128)(2,1)} %fusion.3.h_ref, ...), custom_call_target="tpu_custom_call" | custom-call | flops 7247757312 | bytes 9437184 | tf_op jit(solution)/shard_map/sweep/pallas_call | solution.py:346
  170.4 86.1 %all_to_all.15 = bf16[256,8,768]{2,1,0:T(8,128)(2,1)} all-to-all(bf16[256,8,768]{2,1,0:T(8,128)(2,1)} %bitcast.20), channel_id=1, replica_groups=mesh['lead'=8,'space'=32] {'lead','space'}, dimensions={0} | all-to-all | bytes 6291456 | tf_op jit(solution)/shard_map/all_to_all | solution.py:368
  256.5 4.9 %mix_rows.3 = bf16[8,256,768]{2,1,0:T(8,128)(2,1)} custom-call(bf16[256,256]{1,0:T(8,128)(2,1)} %constant.24.clone.m_ref, bf16[8,256,768]{2,1,0:T(8,128)(2,1)} %bitcast.19), custom_call_target="tpu_custom_call" | custom-call | flops 805306368 | bytes 6291456 | tf_op jit(solution)/shard_map/mix_rows/pallas_call | solution.py:96
Async XLA Ops:
  4.9 90.3 %copy-start = (bf16[1,8,2,128,768]{4,3,2,1,0:T(8,128)(2,1)S(1)}, bf16[1,8,2,128,768]{4,3,2,1,0:T(8,128)(2,1)}, u32[]{:S(2)}) copy-start(bf16[1,8,2,128,768]{4,3,2,1,0:T(8,128)(2,1)} %param.18) | copy-start | bytes 9437188
  4.9 90.3 %copy-start.2 = (bf16[768,128]{1,0:T(8,128)(2,1)S(1)}, bf16[768,128]{1,0:T(8,128)(2,1)}, u32[]{:S(2)}) copy-start(bf16[768,128]{1,0:T(8,128)(2,1)} %dec_ref.1) | copy-start | bytes 589828
  4.9 113.8 %all-to-all-start = ((bf16[256,8,768]{2,1,0:T(8,128)(2,1)}), bf16[256,8,768]{2,1,0:T(8,128)(2,1)}, u32[]{:S(2)}, u32[]{:S(2)}) async-start(bf16[256,8,768]{2,1,0:T(8,128)(2,1)} %bitcast.18), calls=%async_computation | async-start | bytes 6291456 | tf_op jit(solution)/shard_map/all_to_all | solution.py:368
  23.6 9.5 %collective-permute-start = (f32[8,24,128]{2,1,0:T(8,128)}, f32[8,24,128]{2,1,0:T(8,128)S(1)}, u32[]{:S(2)}, u32[]{:S(2)}) collective-permute-start(f32[8,24,128]{2,1,0:T(8,128)} %get-tuple-element.22), channel_id=1, source_target_pairs={{0,1},{1,2},{2,3},{3,0},{4,5},{5,6},{6,7},{7,4},{8,9},{9,10},{10,1... | collective-permute-start | bytes 294920 | tf_op jit(solution)/shard_map/ppermute | solution.py:207
  25.0 13.0 %collective-permute-start.1 = (f32[8,24,128]{2,1,0:T(8,128)}, f32[8,24,128]{2,1,0:T(8,128)S(1)}, u32[]{:S(2)}, u32[]{:S(2)}) collective-permute-start(f32[8,24,128]{2,1,0:T(8,128)} %get-tuple-element.23), channel_id=1, source_target_pairs={{0,2},{1,3},{2,0},{3,1},{4,6},{5,7},{6,4},{7,5},{8,10},{9,11},{10,... | collective-permute-start | bytes 294920 | tf_op jit(solution)/shard_map/ppermute | solution.py:207
  27.4 10.6 %collective-permute-start.2 = (f32[8,24,128]{2,1,0:T(8,128)}, f32[8,24,128]{2,1,0:T(8,128)}, u32[]{:S(2)}, u32[]{:S(2)}) collective-permute-start(f32[8,24,128]{2,1,0:T(8,128)} %get-tuple-element.24), channel_id=1, source_target_pairs={{0,3},{1,0},{2,1},{3,2},{4,7},{5,4},{6,5},{7,6},{8,11},{9,8},{10,9... | collective-permute-start | bytes 294920 | tf_op jit(solution)/shard_map/ppermute | solution.py:207
  33.1 4.9 %copy-start.4 = (f32[8,24,128]{2,1,0:T(8,128)}, f32[8,24,128]{2,1,0:T(8,128)S(1)}, u32[]{:S(2)}) copy-start(f32[8,24,128]{2,1,0:T(8,128)S(1)} %collective-permute-done.refs_1_) | copy-start | bytes 294916
  38.0 0.6 copy-start.5
  40.4 51.5 %collective-permute-start.3 = (f32[4,24,128]{2,1,0:T(8,128)}, f32[4,24,128]{2,1,0:T(8,128)S(1)}, u32[]{:S(2)}, u32[]{:S(2)}) collective-permute-start(f32[4,24,128]{2,1,0:T(8,128)} %get-tuple-element.26), channel_id=1, source_target_pairs={{0,4},{1,5},{2,6},{3,7},{4,8},{5,9},{6,10},{7,11},{8,12},{9,13},{1... | collective-permute-start | bytes 147464 | tf_op jit(solution)/shard_map/ppermute | solution.py:207
  41.7 52.8 %collective-permute-start.4 = (f32[4,24,128]{2,1,0:T(8,128)}, f32[4,24,128]{2,1,0:T(8,128)S(1)}, u32[]{:S(2)}, u32[]{:S(2)}) collective-permute-start(f32[4,24,128]{2,1,0:T(8,128)} %get-tuple-element.27), channel_id=1, source_target_pairs={{0,8},{1,9},{2,10},{3,11},{4,12},{5,13},{6,14},{7,15},{8,16},{9,17... | collective-permute-start | bytes 147464 | tf_op jit(solution)/shard_map/ppermute | solution.py:207
  44.9 52.2 %collective-permute-start.5 = (f32[4,24,128]{2,1,0:T(8,128)}, f32[4,24,128]{2,1,0:T(8,128)S(1)}, u32[]{:S(2)}, u32[]{:S(2)}) collective-permute-start(f32[4,24,128]{2,1,0:T(8,128)} %get-tuple-element.28), channel_id=1, source_target_pairs={{0,12},{1,13},{2,14},{3,15},{4,16},{5,17},{6,18},{7,19},{8,20},{9,... | collective-permute-start | bytes 147464 | tf_op jit(solution)/shard_map/ppermute | solution.py:207
  49.1 52.7 %collective-permute-start.6 = (f32[4,24,128]{2,1,0:T(8,128)}, f32[4,24,128]{2,1,0:T(8,128)S(1)}, u32[]{:S(2)}, u32[]{:S(2)}) collective-permute-start(f32[4,24,128]{2,1,0:T(8,128)} %get-tuple-element.29), channel_id=1, source_target_pairs={{0,16},{1,17},{2,18},{3,19},{4,20},{5,21},{6,22},{7,23},{8,24},{9,... | collective-permute-start | bytes 147464 | tf_op jit(solution)/shard_map/ppermute | solution.py:207
  49.4 52.4 %collective-permute-start.7 = (f32[4,24,128]{2,1,0:T(8,128)}, f32[4,24,128]{2,1,0:T(8,128)S(1)}, u32[]{:S(2)}, u32[]{:S(2)}) collective-permute-start(f32[4,24,128]{2,1,0:T(8,128)} %get-tuple-element.30), channel_id=1, source_target_pairs={{0,20},{1,21},{2,22},{3,23},{4,24},{5,25},{6,26},{7,27},{8,28},{9,... | collective-permute-start | bytes 147464 | tf_op jit(solution)/shard_map/ppermute | solution.py:207
  91.9 11.1 %copy-start.6 = (f32[4,24,128]{2,1,0:T(8,128)}, f32[4,24,128]{2,1,0:T(8,128)S(1)}, u32[]{:S(2)}) copy-start(f32[4,24,128]{2,1,0:T(8,128)S(1)} %collective-permute-done.3.refs_1_) | copy-start | bytes 147460
  91.9 9.9 %collective-permute-start.8 = (f32[4,24,128]{2,1,0:T(8,128)}, f32[4,24,128]{2,1,0:T(8,128)S(1)}, u32[]{:S(2)}, u32[]{:S(2)}) collective-permute-start(f32[4,24,128]{2,1,0:T(8,128)} %get-tuple-element.31), channel_id=1, source_target_pairs={{0,24},{1,25},{2,26},{3,27},{4,28},{5,29},{6,30},{7,31},{8,0},{9,1... | collective-permute-start | bytes 147464 | tf_op jit(solution)/shard_map/ppermute | solution.py:207
  94.5 8.6 %copy-start.7 = (f32[4,24,128]{2,1,0:T(8,128)}, f32[4,24,128]{2,1,0:T(8,128)S(1)}, u32[]{:S(2)}) copy-start(f32[4,24,128]{2,1,0:T(8,128)S(1)} %collective-permute-done.4.refs_2_) | copy-start | bytes 147460
  94.5 7.3 %collective-permute-start.9 = (f32[4,24,128]{2,1,0:T(8,128)}, f32[4,24,128]{2,1,0:T(8,128)S(1)}, u32[]{:S(2)}, u32[]{:S(2)}) collective-permute-start(f32[4,24,128]{2,1,0:T(8,128)} %get-tuple-element.32), channel_id=1, source_target_pairs={{0,28},{1,29},{2,30},{3,31},{4,0},{5,1},{6,2},{7,3},{8,4},{9,5},{1... | collective-permute-start | bytes 147464 | tf_op jit(solution)/shard_map/ppermute | solution.py:207
  97.1 5.9 %copy-start.8 = (f32[4,24,128]{2,1,0:T(8,128)}, f32[4,24,128]{2,1,0:T(8,128)S(1)}, u32[]{:S(2)}) copy-start(f32[4,24,128]{2,1,0:T(8,128)S(1)} %collective-permute-done.5.refs_3_) | copy-start | bytes 147460
  101.8 1.3 copy-start.9
  101.8 0.6 copy-start.10
  101.8 0.6 copy-start.11
  102.4 0.6 copy-start.12
  103.1 29.1 %copy-start.3 = (bf16[256,256]{1,0:T(8,128)(2,1)S(1)}, bf16[256,256]{1,0:T(8,128)(2,1)}, u32[]{:S(2)}) copy-start(bf16[256,256]{1,0:T(8,128)(2,1)} %constant.27.clone) | copy-start | bytes 393220
  118.6 29.4 %all-to-all-start.1 = ((bf16[256,8,128]{2,1,0:T(8,128)(2,1)}), bf16[256,8,128]{2,1,0:T(8,128)(2,1)S(1)}, u32[]{:S(2)}, u32[]{:S(2)}) async-start(bf16[256,8,128]{2,1,0:T(8,128)(2,1)} %bitcast.21), calls=%async_computation.1 | async-start | bytes 1048576 | tf_op jit(solution)/shard_map/all_to_all | solution.py:368
  148.1 0.8 copy-start.1

commit v3 on v2

--- a/solution.py
+++ b/solution.py
@@ -51,25 +51,24 @@
         merid[0, k, :, :, 1, k] = lat_sin
         merid[1, k, :, :, 0, k] = -lat_sin
         merid[1, k, :, :, 1, k] = lat_cos
-    merid = merid.reshape(2 * pair * lat_len, lat_len * 2 * pair)
-    herm = np.zeros((2, pair, lat_len, 2, pair, lat_len))
-    flip = (-np.arange(lat_len)) % lat_len
-    for k in range(pair):
-        for part in range(2):
-            for p in range(lat_len):
-                if k == 0:
-                    herm[part, k, p, part, k, p] += 0.5
-                    herm[part, k, p, part, k, flip[p]] += 0.5 if part == 0 else -0.5
-                else:
-                    herm[part, k, p, part, k, p] = 1.0
-    herm = herm.reshape(2 * pair * lat_len, 2 * pair * lat_len)
+    middle = lat_len // 2
+    order = np.concatenate([np.arange(middle), [middle], np.arange(lat_len - 1, middle, -1)])
+    merid = merid[:, :, order].reshape(2 * pair * lat_len, lat_len * 2 * pair)
+    keep = np.ones((2, pair, lat_len, 1))
+    take = np.zeros((2, pair, lat_len, 1))
+    paired = (order % middle != 0)[:, None]
+    keep[0, 0] = np.where(paired, 0.5, 1.0)
+    take[0, 0] = np.where(paired, 0.5, 0.0)
+    keep[1, 0] = np.where(paired, 0.5, 0.0)
+    take[1, 0] = np.where(paired, -0.5, 0.0)
+    herm = np.stack([keep, take]).reshape(2, 2 * pair * lat_len, 1)
     return {
         "state": zonal(1.0, False).astype(np.float32),
         "force": zonal(gain, True).astype(np.float32),
         "back": zonal(1.0, True).T.astype(np.float32),
         "merid": merid.astype(np.float32),
         "merid_t": merid.T.astype(np.float32),
-        "herm": herm.astype(np.float32),
+        "herm": np.broadcast_to(herm, herm.shape[:2] + (128,)).astype(np.float32),
     }
 
 
@@ -85,7 +84,7 @@
     return pl.CostEstimate(flops=2 * products, transcendentals=0, bytes_accessed=moved)
 
 
-def mix_rows(matrix, array, per_step=2):
+def mix_rows(matrix, array, per_step=4):
     batch, rows, cols = array.shape
 
     def body(m_ref, x_ref, o_ref):
@@ -136,92 +135,47 @@
     )(filter_in, filter_out, jnp.asarray(lift, jnp.bfloat16), jnp.asarray(same, jnp.float32))
 
 
-def pack_outbox(obs_value, obs_weight, obs_index, block_dest, block_count, here, near, far):
+def pack_outbox(obs_value, obs_weight, obs_index, block_dest, block_count, tiles):
     members, rows = obs_value.shape
     blocks = rows // OBS_BLK
-    height = 2 * members + 8
-
-    def body(here_ref, dest_ref, count_ref, value_ref, weight_ref, index_ref, *rest):
-        o_refs, box_ref, seen_ref = rest[:near], rest[near], rest[near + 1]
-        box_ref[...] = jnp.zeros_like(box_ref)
+
+    def body(dest_ref, count_ref, value_ref, weight_ref, index_ref, o_ref, seen_ref):
+        o_ref[...] = jnp.zeros_like(o_ref)
         lane = lax.broadcasted_iota(jnp.int32, (1, OBS_BLK), 1)
-        my_far, my_near = here_ref[0] // near, here_ref[0] % near
-        for t in range(near * far):
+        for t in range(tiles):
             seen_ref[t] = 0
         for b in range(blocks):
             tile = dest_ref[b]
-            slot = (tile % near + near - my_near) % near * far + (tile // near + far - my_far) % far
             rank = seen_ref[tile]
             seen_ref[tile] = rank + 1
             span = slice(b * OBS_BLK, (b + 1) * OBS_BLK)
             weight = jnp.where(lane < count_ref[b], weight_ref[:, span], 0.0)
-            box_ref[slot, pl.ds(pl.multiple_of(rank * members, members), members), :] = (
+            o_ref[tile, pl.ds(pl.multiple_of(rank * members, members), members), :] = (
                 value_ref[:, span] * weight
             )
-            box_ref[slot, pl.ds(2 * members + rank, 1), :] = weight
-            box_ref[slot, pl.ds(2 * members + 2 + rank, 1), :] = index_ref[:, span].astype(jnp.float32)
-        for r in range(near):
-            o_refs[r][...] = box_ref[r * far : (r + 1) * far]
+            o_ref[tile, pl.ds(2 * members + rank, 1), :] = weight
+            o_ref[tile, pl.ds(2 * members + 2 + rank, 1), :] = index_ref[:, span].astype(jnp.float32)
 
     smem = pl.BlockSpec(memory_space=pltpu.SMEM)
     vmem = pl.BlockSpec(memory_space=pltpu.VMEM)
     return pl.pallas_call(
         body,
-        out_shape=[jax.ShapeDtypeStruct((far, height, OBS_BLK), jnp.float32)] * near,
-        in_specs=[smem, smem, smem, vmem, vmem, vmem],
-        out_specs=[vmem] * near,
-        scratch_shapes=[
-            pltpu.VMEM((near * far, height, OBS_BLK), jnp.float32),
-            pltpu.SMEM((near * far,), jnp.int32),
-        ],
+        out_shape=jax.ShapeDtypeStruct((tiles, 2 * members + 8, OBS_BLK), jnp.float32),
+        in_specs=[smem, smem, vmem, vmem, vmem],
+        out_specs=vmem,
+        scratch_shapes=[pltpu.SMEM((tiles,), jnp.int32)],
         name="pack_outbox",
-    )(here, block_dest, block_count, obs_value, obs_weight, obs_index)
-
-
-def regroup(arrays):
-    near, far = len(arrays), arrays[0].shape[0]
-    rest = arrays[0].shape[1:]
-
-    def body(*refs):
-        for q in range(far):
-            for r in range(near):
-                refs[near + q][r] = refs[r][q]
-
-    vmem = pl.BlockSpec(memory_space=pltpu.VMEM)
-    return pl.pallas_call(
-        body,
-        out_shape=[jax.ShapeDtypeStruct((near,) + rest, arrays[0].dtype)] * far,
-        in_specs=[vmem] * near,
-        out_specs=[vmem] * far,
-        name="regroup",
-    )(*arrays)
-
-
-def route(arrays, near, far):
-    def shift(array, by_near, by_far):
-        perm = [
-            (z * near + y, (z + by_far) % far * near + (y + by_near) % near)
-            for z in range(far)
-            for y in range(near)
-        ]
-        return lax.ppermute(array, "space", perm)
-
-    arrays = [arrays[0]] + [shift(arrays[r], r, 0) for r in range(1, near)]
-    arrays = regroup(arrays)
-    return [arrays[0]] + [shift(arrays[q], 0, q) for q in range(1, far)]
+    )(block_dest, block_count, obs_value, obs_weight, obs_index)
 
 
 def level_spectra(received, decoded, matrix):
-    parts, group, height, lanes = (len(received),) + received[0].shape
+    sources, _, lanes = received.shape
+    group = 4
     members, cells, levels = decoded.shape
     wide = 2 * lanes
     span = group * wide
 
-    def body(*refs):
-        got_refs = refs[:parts]
-        dec_ref, mat_ref, o_ref, got_ref, cell_ref, val_ref, acc_ref = refs[parts:]
-        for q in range(parts):
-            got_ref[q * group : (q + 1) * group] = got_refs[q][...]
+    def body(got_ref, dec_ref, mat_ref, o_ref, cell_ref, val_ref, acc_ref):
         acc_ref[...] = jnp.zeros_like(acc_ref)
         cell_iota = lax.broadcasted_iota(jnp.int32, (cells, wide), 0)
         level_iota = lax.broadcasted_iota(jnp.int32, (levels, wide), 0)
@@ -252,7 +206,7 @@
             acc_ref[...] += dot_nt(cell_ref[...], val_ref[...])
             return carry
 
-        lax.fori_loop(0, parts, one_group, 0)
+        lax.fori_loop(0, sources // group, one_group, 0)
         weights = acc_ref[:, :levels]
         for q in range(members):
             forcing = weights * dec_ref[q] - acc_ref[:, (q + 1) * levels : (q + 2) * levels]
@@ -262,17 +216,16 @@
     return pl.pallas_call(
         body,
         out_shape=jax.ShapeDtypeStruct((members, matrix.shape[0], levels), jnp.bfloat16),
-        in_specs=[vmem] * (parts + 2),
+        in_specs=[vmem] * 3,
         out_specs=vmem,
         scratch_shapes=[
-            pltpu.VMEM((parts * group, height, lanes), jnp.float32),
             pltpu.VMEM((cells, 2 * span), jnp.bfloat16),
             pltpu.VMEM(((members + 1) * levels, 2 * span), jnp.bfloat16),
             pltpu.VMEM((cells, (members + 1) * levels), jnp.float32),
         ],
-        cost_estimate=cost(16 * parts * group * wide * cells * levels, 4 * members * cells * levels),
+        cost_estimate=cost(16 * sources * wide * cells * levels, 4 * members * cells * levels),
         name="level_spectra",
-    )(*received, decoded, matrix)
+    )(received, decoded, matrix)
 
 
 def slopes(spectra, merid, mats, bias):
@@ -307,36 +260,45 @@
     )(spectra, merid, mats, bias)
 
 
-def sweep(slope, level_spec, merid, merid_t, herm, mats, decoder):
+def sweep(slope, level_spec, merid, merid_t, herm, mats, decoder, group):
     sections, rows, cols = slope.shape
     _, chunks, _, width = mats.shape
     levels = decoder.shape[1]
     half = rows // 2
 
-    def body(x_ref, f_ref, d_ref, dt_ref, h_ref, w_ref, dec_ref, o_ref, seen_ref, all_ref):
+    def body(x_ref, f_ref, d_ref, dt_ref, h_ref, w_ref, dec_ref, o_ref, z_ref):
         @pl.when(pl.program_id(0) == 0)
         def _():
-            seen_ref[...] = jnp.zeros_like(seen_ref)
-            all_ref[...] = jnp.zeros_like(all_ref)
+            z_ref[...] = jnp.zeros_like(z_ref)
+
+        keep = jnp.concatenate([h_ref[0]] * (width // h_ref.shape[2]), axis=1)
+        take = jnp.concatenate([h_ref[1]] * (width // h_ref.shape[2]), axis=1)
+
+        def hermitian(array):
+            parts = []
+            for g in range(0, rows, group):
+                parts += [array[g + group // 2 : g + group], array[g : g + group // 2]]
+            return keep * array + take * jnp.concatenate(parts, axis=0)
 
         def crossed(array):
+            array = array.astype(jnp.bfloat16)
             re, im = array[:half], array[half:]
             return jnp.concatenate(
                 [jnp.concatenate([re, im], axis=1), jnp.concatenate([im, -re], axis=1)], axis=0
             )
 
+        spans = [slice(c * width, (c + 1) * width) for c in range(chunks)]
         forced = dot(d_ref[...], f_ref[0]).astype(jnp.bfloat16)
-        forced_seen = dot(h_ref[...], forced).astype(jnp.bfloat16)
-        for c in range(chunks):
-            at = slice(c * width, (c + 1) * width)
-            seen = seen_ref[:, at]
-            hid = dot(crossed(seen.astype(jnp.bfloat16)), w_ref[0, c])
-            act = (hid * x_ref[0, :, at]).astype(jnp.bfloat16)
-            grad = dot(crossed(act), w_ref[1, c]).astype(jnp.bfloat16)
-            grad = dot(h_ref[...], grad)
-            seen_ref[:, at] = seen + grad + dot_nt(forced_seen, dec_ref[at])
-            total = all_ref[:, at] + grad + dot_nt(forced, dec_ref[at])
-            all_ref[:, at] = total
+        hids = [
+            dot(crossed(hermitian(z_ref[:, at])), w_ref[0, c]) for c, at in enumerate(spans)
+        ]
+        pushed = [z_ref[:, at] + dot_nt(forced, dec_ref[at]) for at in spans]
+        grads = [
+            dot(crossed(hids[c] * x_ref[0, :, at]), w_ref[1, c]) for c, at in enumerate(spans)
+        ]
+        for c, at in enumerate(spans):
+            total = pushed[c] + hermitian(grads[c])
+            z_ref[:, at] = total
             o_ref[0, :, at] = dot(dt_ref[...], total.astype(jnp.bfloat16)).astype(jnp.bfloat16)
 
     def turn(width):
@@ -352,12 +314,12 @@
             turn(levels),
             square,
             square,
-            square,
+            pl.BlockSpec(herm.shape, lambda t: (0, 0, 0)),
             pl.BlockSpec((2,) + mats.shape[1:], lambda t: (0, 0, 0, 0)),
             pl.BlockSpec((cols, levels), lambda t: (0, 0)),
         ],
         out_specs=turn(cols),
-        scratch_shapes=[pltpu.VMEM((rows, cols), jnp.float32)] * 2,
+        scratch_shapes=[pltpu.VMEM((rows, cols), jnp.float32)],
         cost_estimate=cost(6 * sections * rows * cols * width, 6 * sections * rows * cols),
         name="sweep",
     )(slope, level_spec, merid, merid_t, herm, mats, decoder)
@@ -385,26 +347,34 @@
     member_count, lat_local, lon_len, channels = states.shape[1:]
     tiles = lax.axis_size("space")
     tables = {
-        name: jnp.asarray(table, jnp.bfloat16)
+        name: jnp.asarray(table, jnp.float32 if name == "herm" else jnp.bfloat16)
         for name, table in make_matrices(tiles, lat_local, lon_len).items()
     }
     fields = states.reshape(member_count, lat_local * lon_len, channels)
-    near = math.gcd(tiles, 4)
-    far = tiles // near
-    here = lax.axis_index("space").astype(jnp.int32)
-    spectra = swap(mix_rows(tables["state"], fields), EVERY)
-    outbox = pack_outbox(
-        obs_value[0], obs_weight, obs_index, block_dest[0], block_count[0], here[None], near, far
-    )
-    received = route(outbox, near, far)
+    outbox = pack_outbox(obs_value[0], obs_weight, obs_index, block_dest[0], block_count[0], tiles)
+    received = lax.all_to_all(outbox, "space", split_axis=0, concat_axis=0, tiled=True)
+    mixed = mix_rows(tables["state"], fields)
+    mixed, received = lax.optimization_barrier((mixed, received))
+    spectra = swap(mixed, EVERY)
     decoded = jnp.einsum("mnc,cv->mnv", fields, decoder, preferred_element_type=jnp.float32)
     levels = level_spectra(received, decoded, tables["force"])
     spectra, levels = lax.optimization_barrier((spectra, levels))
     levels = swap(levels, EVERY)
     forward, adjoint = dense_blocks(filter_in, filter_out, 2)
-    herm = jnp.where(here == 0, tables["herm"], jnp.eye(tables["herm"].shape[0], dtype=jnp.bfloat16))
+    plain = np.zeros(tables["herm"].shape, np.float32)
+    plain[0] = 1.0
+    herm = jnp.where(lax.axis_index("space") == 0, tables["herm"], plain)
     slope = slopes(spectra, tables["merid"], forward, filter_bias)
-    swept = sweep(slope, levels, tables["merid"], tables["merid_t"], herm, adjoint, decoder)
+    swept = sweep(
+        slope,
+        levels,
+        tables["merid"],
+        tables["merid_t"],
+        herm,
+        adjoint,
+        decoder,
+        tiles * lat_local,
+    )
     result = mix_rows(tables["back"], swap(swept, EVERY))
     return result.reshape(1, member_count, lat_local, lon_len, channels)
 

time: 262 us -> 245 us (0.935)
  starting transfers between devices: 46.6 us -> 28 us
  waiting for transfers between devices: 57 us -> 70.8 us
  Pallas kernels: 66.2 us -> 54.3 us
    all_to_all x2, waiting for transfers between devices: 3.85 us -> 60.7 us  [swap(): lax.all_to_all(array.reshape(-1, 8, cols), axis, split_axis=0, concat_axi...]
    ppermute x10 -> x0, waiting for transfers between devices: 53.1 us -> none  [shift(): return lax.ppermute(array, 'space', perm)]
    ppermute x10 -> x0, starting transfers between devices: 20.6 us -> none  [shift(): return lax.ppermute(array, 'space', perm)]
    all_to_all x0 -> x1, starting transfers between devices: none -> 12 us  [shards(): lax.all_to_all(outbox, 'space', split_axis=0, concat_axis=0, tiled=True)]
    all_to_all x0 -> x1, waiting for transfers between devices: none -> 10.1 us  [shards(): lax.all_to_all(outbox, 'space', split_axis=0, concat_axis=0, tiled=True)]
    all_to_all x2, starting transfers between devices: 26 us -> 16 us  [swap(): lax.all_to_all(array.reshape(-1, 8, cols), axis, split_axis=0, concat_axi...]
    pallas_call x1, Pallas kernels: 21.5 us -> 14.1 us  [sweep(): pl.pallas_call(body, out_shape=jax.ShapeDtypeStruct((sections, rows, cols...]
  transfers between devices with their start and end apart: 12 -> 3, of which waited for: 6 -> 3; matrix products, arithmetic and copies ran while one was open for 1% -> 1% of each run, Pallas kernels for 13% -> 14%
where the time goes in v3:
time: 245 us
  blocking collectives  86.2 us (35%)
  waiting for transfers between devices  70.8 us (29%)
  Pallas kernels  54.3 us (22%)
  starting transfers between devices  28 us (11%)
  matrix products  2.88 us (1%)
    all_to_all x1, blocking collectives, swap(): lax.all_to_all(array.reshape(-1, 8, cols), axis, split_axis=0, concat_axi...  86.2 us
    all_to_all x2, waiting for transfers between devices, swap(): lax.all_to_all(array.reshape(-1, 8, cols), axis, split_axis=0, concat_axi...  60.7 us
    all_to_all x2, starting transfers between devices, swap(): lax.all_to_all(array.reshape(-1, 8, cols), axis, split_axis=0, concat_axi...  16 us
    pallas_call x1, Pallas kernels, level_spectra(): pl.pallas_call(body, out_shape=jax.ShapeDtypeStruct((members, matrix.shap...  15.4 us
    pallas_call x1, Pallas kernels, sweep(): pl.pallas_call(body, out_shape=jax.ShapeDtypeStruct((sections, rows, cols...  14.1 us
    all_to_all x1, starting transfers between devices, shards(): lax.all_to_all(outbox, 'space', split_axis=0, concat_axis=0, tiled=True)  12 us
    pallas_call x1, Pallas kernels, slopes(): pl.pallas_call(body, out_shape=jax.ShapeDtypeStruct(spectra.shape, jnp.fl...  11.4 us
    all_to_all x1, waiting for transfers between devices, shards(): lax.all_to_all(outbox, 'space', split_axis=0, concat_axis=0, tiled=True)  10.1 us
  transfers between devices with their start and end apart: 3, of which 3 were waited for; matrix products, arithmetic and copies ran while one was open for 1% of the time, Pallas kernels for 14%

profile of v3, /device:TPU:1, one launch (start us, length us, event | category | flops | bytes accessed | tf_op | source)
XLA Modules:
  0.0 244.5 jit_solution(9895173116076542252)
XLA Ops:
  0.0 1.8 pack_outbox.1
  1.8 12.0 %all-to-all-start = ((f32[32,24,128]{2,1,0:T(8,128)}), f32[32,24,128]{2,1,0:T(8,128)S(1)}, u32[]{:S(2)}, u32[]{:S(2)}) async-start(f32[32,24,128]{2,1,0:T(8,128)} %pack_outbox.1), calls=%async_computation | async-start | bytes 786432 | tf_op jit(solution)/shard_map/all_to_all | solution.py:355
  13.9 3.7 %mix_rows.2 = bf16[8,256,768]{2,1,0:T(8,128)(2,1)} custom-call(bf16[256,256]{1,0:T(8,128)(2,1)} %constant.24.clone.m_ref, bf16[8,256,768]{2,1,0:T(8,128)(2,1)} %bitcast.15), custom_call_target="tpu_custom_call" | custom-call | flops 805306368 | bytes 6291456 | tf_op jit(solution)/shard_map/mix_rows/pallas_call | solution.py:95
  17.6 10.1 %all-to-all-done.got_ref = f32[32,24,128]{2,1,0:T(8,128)S(1)} async-done(((f32[32,24,128]{2,1,0:T(8,128)}), f32[32,24,128]{2,1,0:T(8,128)S(1)}, u32[]{:S(2)}, u32[]{:S(2)}) %all-to-all-start) | async-done | bytes 393248 | tf_op jit(solution)/shard_map/all_to_all | solution.py:355
  27.7 0.0 copy-start.2
  27.7 0.0 copy-start
  27.7 0.7 copy-done.2
  28.4 10.3 %all-to-all-start.1 = ((bf16[256,8,768]{2,1,0:T(8,128)(2,1)}), bf16[256,8,768]{2,1,0:T(8,128)(2,1)}, u32[]{:S(2)}, u32[]{:S(2)}) async-start(bf16[256,8,768]{2,1,0:T(8,128)(2,1)} %bitcast.17), calls=%async_computation.1 | async-start | bytes 6291456 | tf_op jit(solution)/shard_map/all_to_all | solution.py:330
  38.7 0.0 copy-done
  38.7 2.9 %fusion.dec_ref = f32[8,256,128]{2,1,0:T(8,128)} fusion(bf16[8,256,768]{2,1,0:T(8,128)(2,1)S(1)} %bitcast.16, bf16[768,128]{1,0:T(8,128)(2,1)} %dec_ref.1), kind=kOutput, calls=%fused_computation | convolution fusion | flops 402653184 | bytes 4390912 | tf_op jit(solution)/shard_map/mnc,cv->mnv/dot_general | solution.py:359
  41.6 0.0 copy-start.3
  41.6 0.0 copy-start.4
  41.6 15.4 %level_spectra.1 = bf16[8,256,128]{2,1,0:T(8,128)(2,1)} custom-call(f32[32,24,128]{2,1,0:T(8,128)} %copy-done.2, f32[8,256,128]{2,1,0:T(8,128)} %fusion.dec_ref, bf16[256,256]{1,0:T(8,128)(2,1)} %constant.25.clone.mat_ref), custom_call_target="tpu_custom_call" | custom-call | flops 8589934592 | bytes 1048576 | tf_op jit(solution)/shard_map/level_spectra/pallas_call | solution.py:216
  57.0 57.0 %all-to-all-done.1 = bf16[256,8,768]{2,1,0:T(8,128)(2,1)} async-done(((bf16[256,8,768]{2,1,0:T(8,128)(2,1)}), bf16[256,8,768]{2,1,0:T(8,128)(2,1)}, u32[]{:S(2)}, u32[]{:S(2)}) %all-to-all-start.1) | async-done | bytes 3145760 | tf_op jit(solution)/shard_map/all_to_all | solution.py:330
  114.0 5.8 %all-to-all-start.2 = ((bf16[256,8,128]{2,1,0:T(8,128)(2,1)}), bf16[256,8,128]{2,1,0:T(8,128)(2,1)S(1)}, u32[]{:S(2)}, u32[]{:S(2)}) async-start(bf16[256,8,128]{2,1,0:T(8,128)(2,1)} %bitcast.20), calls=%async_computation.2 | async-start | bytes 1048576 | tf_op jit(solution)/shard_map/all_to_all | solution.py:330
  119.8 4.0 %dense_blocks.1 = (bf16[1,2,768,384]{3,2,1,0:T(8,128)(2,1)}, bf16[2,2,768,384]{3,2,1,0:T(8,128)(2,1)}) custom-call(bf16[2,8,96,96]{3,2,1,0:T(8,128)(2,1)} %in_ref.1, bf16[2,8,96,96]{3,2,1,0:T(8,128)(2,1)} %out_ref.1, bf16[384,96]{1,0:T(8,128)(2,1)} %constant.30.clone.lift_ref, f32[384,384]{1,0:T(8,128)} %constant.31.clone.same_ref), custom_call_target="tpu_custom_call" | custom-call | flops 339738624 | bytes 1769472 | tf_op jit(solution)/shard_map/dense_blocks/pallas_call | solution.py:125
  123.8 0.0 copy-done.3
  123.8 0.0 copy-done.4
  123.8 0.7 broadcast_select_fusion.h_ref
  124.6 11.4 %slopes.1.x_ref = f32[8,256,768]{2,1,0:T(8,128)} custom-call(bf16[8,256,768]{2,1,0:T(8,128)(2,1)} %bitcast.5.x_ref, bf16[256,256]{1,0:T(8,128)(2,1)} %constant.27.clone.d_ref, bf16[1,2,768,384]{3,2,1,0:T(8,128)(2,1)} %get-tuple-element.14.w_ref, f32[2,768]{1,0:T(2,128)} %b_ref.1), custom_call_target="tpu_custom_call" | custom-call | flops 3623878656 | bytes 9437184 | tf_op jit(solution)/shard_map/slopes/pallas_call | solution.py:247
  135.9 3.7 %all-to-all-done.2 = bf16[256,8,128]{2,1,0:T(8,128)(2,1)S(1)} async-done(((bf16[256,8,128]{2,1,0:T(8,128)(2,1)}), bf16[256,8,128]{2,1,0:T(8,128)(2,1)S(1)}, u32[]{:S(2)}, u32[]{:S(2)}) %all-to-all-start.2) | async-done | bytes 524320 | tf_op jit(solution)/shard_map/all_to_all | solution.py:330
  139.7 0.0 copy-start.1
  139.7 0.8 copy-done.1
  140.5 14.1 %sweep.1 = bf16[8,256,768]{2,1,0:T(8,128)(2,1)} custom-call(f32[8,256,768]{2,1,0:T(8,128)} %slopes.1.x_ref, bf16[8,256,128]{2,1,0:T(8,128)(2,1)} %bitcast.21, bf16[256,256]{1,0:T(8,128)(2,1)} %constant.27.clone.d_ref, bf16[256,256]{1,0:T(8,128)(2,1)} %constant.28.clone.dt_ref, f32[2,256,128]{2,1,0:T(8,128)} %broadcast_select_fusion.h_ref, ...), custom_call_target="tpu_custom_call" | custom-call | flops 7247757312 | bytes 9437184 | tf_op jit(solution)/shard_map/sweep/pallas_call | solution.py:308
  154.6 86.2 %all_to_all.20 = bf16[256,8,768]{2,1,0:T(8,128)(2,1)} all-to-all(bf16[256,8,768]{2,1,0:T(8,128)(2,1)} %bitcast.19), channel_id=1, replica_groups=mesh['lead'=8,'space'=32] {'lead','space'}, dimensions={0} | all-to-all | bytes 6291456 | tf_op jit(solution)/shard_map/all_to_all | solution.py:330
  240.8 3.7 %mix_rows.3 = bf16[8,256,768]{2,1,0:T(8,128)(2,1)} custom-call(bf16[256,256]{1,0:T(8,128)(2,1)} %constant.26.clone.m_ref, bf16[8,256,768]{2,1,0:T(8,128)(2,1)} %bitcast.18), custom_call_target="tpu_custom_call" | custom-call | flops 805306368 | bytes 6291456 | tf_op jit(solution)/shard_map/mix_rows/pallas_call | solution.py:95
Async XLA Ops:
  1.8 25.9 %all-to-all-start = ((f32[32,24,128]{2,1,0:T(8,128)}), f32[32,24,128]{2,1,0:T(8,128)S(1)}, u32[]{:S(2)}, u32[]{:S(2)}) async-start(f32[32,24,128]{2,1,0:T(8,128)} %pack_outbox.1), calls=%async_computation | async-start | bytes 786432 | tf_op jit(solution)/shard_map/all_to_all | solution.py:355
  27.7 0.7 copy-start.2
  27.7 11.0 %copy-start = (bf16[1,8,2,128,768]{4,3,2,1,0:T(8,128)(2,1)S(1)}, bf16[1,8,2,128,768]{4,3,2,1,0:T(8,128)(2,1)}, u32[]{:S(2)}) copy-start(bf16[1,8,2,128,768]{4,3,2,1,0:T(8,128)(2,1)} %param.19) | copy-start | bytes 9437188
  28.4 85.6 %all-to-all-start.1 = ((bf16[256,8,768]{2,1,0:T(8,128)(2,1)}), bf16[256,8,768]{2,1,0:T(8,128)(2,1)}, u32[]{:S(2)}, u32[]{:S(2)}) async-start(bf16[256,8,768]{2,1,0:T(8,128)(2,1)} %bitcast.17), calls=%async_computation.1 | async-start | bytes 6291456 | tf_op jit(solution)/shard_map/all_to_all | solution.py:330
  41.6 82.2 %copy-start.3 = (f32[2,256,128]{2,1,0:T(8,128)S(1)}, f32[2,256,128]{2,1,0:T(8,128)}, u32[]{:S(2)}) copy-start(f32[2,256,128]{2,1,0:T(8,128)} %constant.29.clone) | copy-start | bytes 786436
  41.6 82.2 %copy-start.4 = (f32[2,256,128]{2,1,0:T(8,128)S(1)}, f32[2,256,128]{2,1,0:T(8,128)}, u32[]{:S(2)}) copy-start(f32[2,256,128]{2,1,0:T(8,128)} %constant.32.clone) | copy-start | bytes 786436
  114.0 25.7 %all-to-all-start.2 = ((bf16[256,8,128]{2,1,0:T(8,128)(2,1)}), bf16[256,8,128]{2,1,0:T(8,128)(2,1)S(1)}, u32[]{:S(2)}, u32[]{:S(2)}) async-start(bf16[256,8,128]{2,1,0:T(8,128)(2,1)} %bitcast.20), calls=%async_computation.2 | async-start | bytes 1048576 | tf_op jit(solution)/shard_map/all_to_all | solution.py:330
  139.7 0.8 copy-start.1
